TPU v7x, 32 devices: a whole 2x2x4 slice. The times are simulated.
32 devices in a mesh: rows: 4 (over z), keys: 8 (over y, x, core).
Axes of the slice: x: 2, y: 2, z: 4, core: 2. Of those that a mesh axis runs over, the one named last changes fastest.
Arguments:
- tokens: bfloat16 [2, 4, 2048, 768], P(None, 'rows', 'keys'), may hold values from -6 to 6
- prev_logits: bfloat16 [2, 4, 12, 2048, 2048], P(None, 'rows', None, 'keys'), may hold values from -6 to 6
- segments: int32 [2, 4, 2048], P(None, 'rows'), may hold values from 0 to 63, as said below
- out_cot: bfloat16 [2, 4, 2048, 768], P(None, 'rows', 'keys'), may hold values from -6 to 6
- master_mat: float32 [8, 768, 1152], P('rows', None, 'keys'), may hold values from -6 to 6
- mom1_mat: float32 [8, 768, 1152], P('rows', None, 'keys'), may hold values from -38.4 to 38.4
- mom2_mat: float32 [8, 768, 1152], P('rows', None, 'keys'), as said below
- eigen_bases: float32 [8, 768, 768], P('rows'), may hold values from -1 to 1
- master_small: float32 [8, 1152], P('rows', 'keys'), may hold values from -2 to 2
- mom1_small: float32 [8, 1152], P('rows', 'keys'), may hold values from -38.4 to 38.4
- mom2_small: float32 [8, 1152], P('rows', 'keys'), as said below
- owners: int32 [8], replicated, may hold values from 0 to 7, as said below
- step_count: int32 [1], replicated, may hold values from 2 to 20
Outputs:
- out_hidden: bfloat16 [2, 4, 2048, 768], P(None, 'rows', 'keys')
- logits: bfloat16 [2, 4, 12, 2048, 2048], P(None, 'rows', None, 'keys')
- grad_tokens: bfloat16 [2, 4, 2048, 768], P(None, 'rows', 'keys')
- grad_prev: bfloat16 [2, 4, 12, 2048, 2048], P(None, 'rows', None, 'keys')
- grad_mat: float32 [8, 768, 1152], P('rows', None, 'keys')
- new_mom1_mat: float32 [8, 768, 1152], P('rows', None, 'keys')
- new_mom2_mat: float32 [8, 768, 1152], P('rows', None, 'keys')
- new_master_mat: float32 [8, 768, 1152], P('rows', None, 'keys')
- copy_mat: bfloat16 [8, 768, 1152], P('rows', None, 'keys')
- grad_small: float32 [8, 1152], P('rows', 'keys')
- new_mom1_small: float32 [8, 1152], P('rows', 'keys')
- new_mom2_small: float32 [8, 1152], P('rows', 'keys')
- new_master_small: float32 [8, 1152], P('rows', 'keys')
- copy_small: bfloat16 [8, 1152], P('rows', 'keys')
Inputs may be any that keep to these rules, and one draw needn't show every extreme that they name: `segments`: in every packed row the ids start at 0 and rise by one at the first slot of each document; documents start only at multiples of 32 slots; a quarter of a row is wholly inside one document with probability g / 3 for rows index g, and two such quarters side by side belong to the same document; every other quarter starts a new document at its first slot and is cut at each further multiple of 32 with probability one half; the first row of the first micro-batch holds 64 documents. `owners`: A permutation. `mom2_mat`: Positive. `mom2_small`: Positive.
All inputs are finite; a program needn't handle non-finite values.
Results may differ from a plain program's by a relative error of at most 0.025.
Values may be sent and summed in bfloat16 or wider, within the bound.
A program may use at most 448 MiB of HBM per device.

v0:
```python
import functools
import math

import jax
import jax.numpy as jnp
from jax import lax
from jax.experimental import pallas as pl
from jax.experimental.pallas import tpu as pltpu
from jax.sharding import PartitionSpec as P

MODEL_WIDTH = 768
H = 12
HD = 64
FF = 3072
BLOCK_COLUMNS = 1152
GAIN_ROW_WIDTH = 1152

EPS_NORM = 1e-06
BETA_ONE = 0.95
BETA_TWO = 0.95
EPS_ADAM = 1e-08
DECAY = 0.01
RATE_SMALL = 0.3
NEG_BIG = -1e30
NEG_FLOOR = -1e29
HIGHEST_PREC = lax.Precision.HIGHEST
MESH = pl.DeviceIdType.MESH
F32 = jnp.float32
BF16 = jnp.bfloat16
ANY = pl.BlockSpec(memory_space=pl.ANY)
VMEM_SPEC = pl.BlockSpec(memory_space=pltpu.VMEM)
EXT = 16
EARLY = 2
PER = 3
VMEM_LIMIT = 60 << 20


def layer_norm(value):
    mean_val = jnp.mean(value, axis=-1, keepdims=True)
    centered = value - mean_val
    inv_dev = lax.rsqrt(jnp.mean(centered * centered, axis=-1, keepdims=True) + EPS_NORM)
    return (centered * inv_dev, inv_dev)


def norm_back(grad_in, normed, inv_dev, gain):
    scaled = grad_in * gain
    return inv_dev * (
        scaled
        - jnp.mean(scaled, axis=-1, keepdims=True)
        - normed * jnp.mean(scaled * normed, axis=-1, keepdims=True)
    )


def inverse_order(owners):
    slot_index_list = jnp.arange(owners.shape[0], dtype=jnp.int32)
    matches = (owners[None, :] == slot_index_list[:, None]).astype(jnp.int32)
    return jnp.sum(matches * slot_index_list[None, :], axis=1)


def column_rates(columns):
    inner = MODEL_WIDTH ** (-0.5)
    return jnp.where(
        columns < 3 * MODEL_WIDTH,
        inner,
        jnp.where(
            columns < 4 * MODEL_WIDTH,
            4.0 * inner,
            jnp.where(columns < 4 * MODEL_WIDTH + FF, inner, FF ** (-0.5)),
        ),
    )


def dot_f32(left, right, contract):
    return lax.dot_general(left, right, (contract, ((), ())), preferred_element_type=F32)


class Place:
    def __init__(self, side_y, side_x, rows):
        self.Y, self.X, self.R = side_y, side_x, rows
        key = lax.axis_index("keys")
        self.key = key
        self.r = lax.axis_index("rows")
        self.c = lax.rem(key, 2)
        self.x = lax.rem(key // 2, side_x)
        self.y = key // (2 * side_x)

    def keyof(self, y, x, c):
        return (y * self.X + x) * 2 + c

    def xo(self, d):
        return lax.rem(self.x + d, self.X)

    def yo(self, d):
        return lax.rem(self.y + d, self.Y)

    def ro(self, d):
        return lax.rem(self.r + d, self.R)

    def x_peer(self, d):
        return {"keys": self.keyof(self.y, self.xo(d), self.c)}

    def y_peer(self, d):
        return {"keys": self.keyof(self.yo(d), self.x, self.c)}

    def core_peer(self):
        return {"keys": self.keyof(self.y, self.x, 1 - self.c)}

    def z_peer(self, d):
        return {"rows": self.ro(d)}

    def announce(self, with_z):
        peers = [self.core_peer()]
        peers += [self.x_peer(d) for d in range(1, self.X)]
        peers += [self.y_peer(d) for d in range(1, self.Y)]
        if with_z:
            peers += [self.z_peer(d) for d in range(1, self.R)]
        sem = pltpu.get_barrier_semaphore()
        for peer in peers:
            pl.semaphore_signal(sem, inc=1, device_id=peer, device_id_type=MESH)
        self.greeted = len(peers)

    def meet(self):
        pl.semaphore_wait(pltpu.get_barrier_semaphore(), self.greeted)

    def barrier(self, with_z):
        self.announce(with_z)
        self.meet()


def remote(src, dst, send_sem, recv_sem, peer):
    return pltpu.make_async_remote_copy(
        src_ref=src,
        dst_ref=dst,
        send_sem=send_sem,
        recv_sem=recv_sem,
        device_id=peer,
        device_id_type=MESH,
    )


def sems_per_item(Y, X):
    return (X - 1) + (Y - 1) + 1


class Gather:
    def __init__(self, place, own, buf, send, recv, base, x_first):
        p = place
        self.sent = []
        n = sems_per_item(p.Y, p.X)
        idx = iter(range(base, base + n))
        first = [(p.x_peer(d)) for d in range(1, p.X)] if x_first else [p.y_peer(d) for d in range(1, p.Y)]
        second = [p.y_peer(d) for d in range(1, p.Y)] if x_first else [p.x_peer(d) for d in range(1, p.X)]
        line = buf.at[p.y, :, p.c] if x_first else buf.at[:, p.x, p.c]
        plane = buf.at[:, :, p.c]
        mine = buf.at[p.y, p.x, p.c]
        self.one = []
        for peer in first:
            i = next(idx)
            self.one.append(remote(own, mine, send.at[i], recv.at[i], peer))
        self.two = []
        for peer in second:
            i = next(idx)
            self.two.append(remote(line, line, send.at[i], recv.at[i], peer))
        i = next(idx)
        self.three = [remote(plane, plane, send.at[i], recv.at[i], p.core_peer())]

    def start1(self):
        for copy in self.one:
            copy.start()

    def start2(self):
        for copy in self.one:
            copy.wait_recv()
        for copy in self.two:
            copy.start()

    def start3(self):
        for copy in self.two:
            copy.wait_recv()
        for copy in self.three:
            copy.start()

    def finish(self):
        for copy in self.three:
            copy.wait_recv()
        for copy in self.one + self.two + self.three:
            copy.wait_send()


def gather_weights_kernel(
    Y, X, R, owners, w_ref, ext_ref, x_ref, wt_out, first_out, last_out, ext_out, xg_out,
    zbuf, zext, stage, sext, wlow, zsend, zrecv, send, recv, loc,
):
    p = Place(Y, X, R)
    slots_here = w_ref.shape[0]
    blocks = zbuf.shape[0]
    early = wt_out.shape[0]
    micro = x_ref.shape[0]
    n = sems_per_item(Y, X)
    p.announce(True)
    wlow[...] = w_ref[...].astype(BF16)
    p.meet()
    here = pl.ds(p.r * slots_here, slots_here)

    def hop(src, step, own):
        there = pl.ds(src * slots_here, slots_here)
        way = (step + 1) // 2
        peer = {"rows": p.r + step}
        return [
            remote(wlow if own else zbuf.at[there], zbuf.at[there], zsend.at[way, src, 0], zrecv.at[src, 0], peer),
            remote(ext_ref if own else zext.at[src], zext.at[src], zsend.at[way, src, 1], zrecv.at[src, 1], peer),
        ]

    def can(step):
        return p.r < R - 1 if step > 0 else p.r > 0

    def pass_on(dist, act):
        for step in (1, -1):
            src = p.r - step * dist

            @pl.when((src >= 0) & (src < R) & can(step))
            def _():
                for copy in hop(src, step, dist == 0):
                    act(copy)

    def arrived(dist):
        for step in (1, -1):
            src = p.r - step * dist

            @pl.when((src >= 0) & (src < R))
            def _():
                for copy in hop(src, step, False):
                    copy.wait_recv()

    pass_on(0, lambda copy: copy.start())
    xitems = []
    xlocal = []
    for m in range(micro):
        item = Gather(p, x_ref.at[m], xg_out.at[m], send, recv, m * n, m % 2 == 0)
        item.start1()
        xitems.append(item)
        copy = pltpu.make_async_copy(x_ref.at[m], xg_out.at[m, p.y, p.x, p.c], loc.at[m])
        copy.start()
        xlocal.append(copy)
    wl = pltpu.make_async_copy(wlow, zbuf.at[here], loc.at[micro])
    wl.start()
    el = pltpu.make_async_copy(ext_ref, zext.at[p.r], loc.at[micro + 1])
    el.start()
    for m in range(micro):
        xlocal[m].wait()
        xitems[m].start2()
    for dist in range(1, R):
        arrived(dist)
        pass_on(dist, lambda copy: copy.start())
    wl.wait()
    el.wait()
    sext[...] = jnp.sum(zext[...].astype(F32), axis=0).astype(BF16)

    def reorder(b, carry):
        stage[b] = zbuf[owners[b]]
        return carry

    lax.fori_loop(0, blocks, reorder, 0)
    base = micro * n
    eitem = Gather(p, sext, ext_out, send, recv, base, True)
    base += n
    lcopies = []
    items = []
    for b in range(early):
        item = Gather(p, stage.at[b], wt_out.at[b], send, recv, base, b % 2 == 0)
        base += n
        item.start1()
        items.append(item)
        copy = pltpu.make_async_copy(stage.at[b], wt_out.at[b, p.y, p.x, p.c], loc.at[micro + 3 + b])
        copy.start()
        lcopies.append(copy)
    eitem.start1()
    ecopy = pltpu.make_async_copy(sext, ext_out.at[p.y, p.x, p.c], loc.at[micro + 2])
    ecopy.start()
    late = (blocks - early) // 2
    rest = [
        pltpu.make_async_copy(stage.at[pl.ds(early + i * late, late)], out, loc.at[micro + 3 + early + i])
        for i, out in enumerate((first_out, last_out))
    ]
    for copy in rest:
        copy.start()
    for m in range(micro):
        xitems[m].start3()
    for b in range(early):
        lcopies[b].wait()
        items[b].start2()
    ecopy.wait()
    eitem.start2()
    for b in range(early):
        items[b].start3()
    eitem.start3()
    for item in xitems + [eitem] + items:
        item.finish()
    for dist in range(R):
        pass_on(dist, lambda copy: copy.wait_send())
    for copy in rest:
        copy.wait()


def gather_weights(mesh_dims, owners, w_own, ext, x_own):
    Y, X, R = mesh_dims
    slots_here, n, width = w_own.shape
    micro, tok = x_own.shape[:2]
    blocks = slots_here * R
    total = sems_per_item(Y, X) * (micro + 1 + EARLY)
    return pl.pallas_call(
        functools.partial(gather_weights_kernel, Y, X, R),
        out_shape=(
            jax.ShapeDtypeStruct((EARLY, Y, X, 2, n, width), BF16),
            jax.ShapeDtypeStruct(((blocks - EARLY) // 2, n, width), BF16),
            jax.ShapeDtypeStruct(((blocks - EARLY) // 2, n, width), BF16),
            jax.ShapeDtypeStruct((Y, X, 2, EXT, width), BF16),
            jax.ShapeDtypeStruct((micro, Y, X, 2, tok, width), BF16),
        ),
        in_specs=[pl.BlockSpec(memory_space=pltpu.SMEM), VMEM_SPEC, VMEM_SPEC, VMEM_SPEC],
        out_specs=(ANY,) * 5,
        scratch_shapes=[
            pltpu.VMEM((blocks, n, width), BF16),
            pltpu.VMEM((R, EXT, width), BF16),
            pltpu.VMEM((blocks, n, width), BF16),
            pltpu.VMEM((EXT, width), BF16),
            pltpu.VMEM(w_own.shape, BF16),
            pltpu.SemaphoreType.DMA((2, R, 2)),
            pltpu.SemaphoreType.DMA((R, 2)),
            pltpu.SemaphoreType.DMA((total,)),
            pltpu.SemaphoreType.DMA((total,)),
            pltpu.SemaphoreType.DMA((micro + 5 + EARLY,)),
        ],
        compiler_params=pltpu.CompilerParams(
            collective_id=1, has_side_effects=True, vmem_limit_bytes=VMEM_LIMIT
        ),
        name="gather_weights",
    )(owners, w_own, ext, x_own)


class Scatter:
    def __init__(self, place, parts, accs, r1s, r2s, r3s, send, recv, loc, base, lbase, y_first, merge):
        p = place
        self.p, self.y_first, self.merge = p, y_first, merge
        self.accs, self.r1s, self.r2s, self.r3s = accs, r1s, r2s, r3s
        self.count = len(parts)
        n = sems_per_item(p.Y, p.X) * len(parts)
        idx = iter(range(base, base + n))
        self.zero, self.one, self.two, self.three = [], [], [], []
        for t, part in enumerate(parts):
            i = next(idx)
            self.zero.append(pltpu.make_async_copy(part.at[:, :, p.c], accs[t], loc.at[lbase + t]))
            self.one.append(remote(part.at[:, :, 1 - p.c], r1s[t], send.at[i], recv.at[i], p.core_peer()))
            if y_first:
                for d in range(1, p.Y):
                    i = next(idx)
                    self.two.append(
                        remote(accs[t].at[p.yo(d)], r2s[t].at[d - 1], send.at[i], recv.at[i], p.y_peer(d))
                    )
                for d in range(1, p.X):
                    i = next(idx)
                    self.three.append(
                        remote(accs[t].at[p.y, p.xo(d)], r3s[t].at[d - 1], send.at[i], recv.at[i], p.x_peer(d))
                    )
            else:
                for d in range(1, p.X):
                    i = next(idx)
                    self.two.append(
                        remote(accs[t].at[:, p.xo(d)], r2s[t].at[d - 1], send.at[i], recv.at[i], p.x_peer(d))
                    )
                for d in range(1, p.Y):
                    i = next(idx)
                    self.three.append(
                        remote(accs[t].at[p.yo(d), p.x], r3s[t].at[d - 1], send.at[i], recv.at[i], p.y_peer(d))
                    )

    def start1(self):
        for copy in self.zero + self.one:
            copy.start()

    def start2(self):
        p = self.p
        for copy in self.zero:
            copy.wait()
        for copy in self.one:
            copy.wait_recv()

        def body(i, carry):
            y, x = i // p.X, lax.rem(i, p.X)
            self.merge([a.at[y, x] for a in self.accs], [r.at[y, x] for r in self.r1s])
            return carry

        lax.fori_loop(0, p.Y * p.X, body, 0)
        for copy in self.two:
            copy.start()

    def start3(self):
        p = self.p
        for copy in self.two:
            copy.wait_recv()
        if self.y_first:
            for d in range(1, p.Y):

                def body(x, carry, d=d):
                    self.merge([a.at[p.y, x] for a in self.accs], [r.at[d - 1, x] for r in self.r2s])
                    return carry

                lax.fori_loop(0, p.X, body, 0)
        else:
            for d in range(1, p.X):

                def body(y, carry, d=d):
                    self.merge([a.at[y, p.x] for a in self.accs], [r.at[d - 1, y] for r in self.r2s])
                    return carry

                lax.fori_loop(0, p.Y, body, 0)
        for copy in self.three:
            copy.start()

    def finish(self):
        p = self.p
        for copy in self.three:
            copy.wait_recv()
        mine = [a.at[p.y, p.x] for a in self.accs]
        for d in range(1, p.X if self.y_first else p.Y):
            self.merge(mine, [r.at[d - 1] for r in self.r3s])
        return mine

    def drain(self):
        for copy in self.one + self.two + self.three:
            copy.wait_send()


def merge_sum(into, other):
    a, b = into[0], other[0]
    a[...] = (a[...].astype(F32) + b[...].astype(F32)).astype(BF16)


def merge_soft(into, other):
    (va, sa), (vb, sb) = into, other
    ta, tb = sa[...], sb[...]
    heads = ta.shape[0] // 2
    top_a, top_b = ta[:heads], tb[:heads]
    top = jnp.maximum(top_a, top_b)
    wa, wb = jnp.exp(top_a - top), jnp.exp(top_b - top)
    sa[...] = jnp.concatenate([top, wa * ta[heads:] + wb * tb[heads:]], axis=0)
    for h in range(heads):
        rows = slice(h * HD, (h + 1) * HD)
        va[rows, :] = (
            va[rows, :].astype(F32) * wa[h : h + 1] + vb[rows, :].astype(F32) * wb[h : h + 1]
        ).astype(BF16)


def scatter_scratch(Y, X, items, shape, dtype, y_first_of):
    most = max((Y - 1) * X, (X - 1) * Y)
    return [
        pltpu.VMEM((items, Y, X) + shape, dtype),
        pltpu.VMEM((items, Y, X) + shape, dtype),
        pltpu.VMEM((items, max(Y, X) - 1, max(Y, X)) + shape, dtype),
        pltpu.VMEM((items, max(Y, X) - 1) + shape, dtype),
    ]


GROUP = 3
STAT_ROWS = 8


def middle_kernel(Y, X, R, blocks, pieces, *refs):
    o_ref, st_ref, x_ref, cot_ref, vec_ref, bu_ref = refs[:6]
    refs = refs[6:]
    count = 2 * Y * X if pieces else 1
    w_refs, refs = refs[:count], refs[count:]
    out_ref, datt_out, stat_out, dz_ref, dvec_ref, dbu_ref = refs[:6]
    refs = refs[6:]
    if pieces:
        send_a, keep_a, send_b, keep_b = refs[:4]
        refs = refs[4:]
    else:
        (dw_out,) = refs[:1]
        refs = refs[1:]
    (
        oa, o1, o2, o3, sa, s1, s2, s3, send, recv, loc, gsend, grecv, gloc, wsem, wsend, wrecv, dwsem,
        w, att, attk, low, hid, dpre, slope, df, da, n1, n2, datt, stat, invs_ref, dw,
    ) = refs[:33]
    if pieces:
        core_acc, core_in, csend, crecv = refs[33:]
    p = Place(Y, X, R)
    micro, tok, width = x_ref.shape
    groups = st_ref.shape[1]
    rows = GROUP * HD
    bo, g1, e1, bd, g2, e2 = (vec_ref[i : i + 1] for i in range(6))
    p.announce(False)
    stat[...] = jnp.zeros_like(stat)
    wide = width
    parts = FF // wide
    wcopies, wremote = [], []
    if pieces:
        half, piece = w_refs[0].shape[:2]
        for t in range(2):
            for dy in range(Y):
                for dx in range(X):
                    src = w_refs[(t * Y + dy) * X + dx]
                    key = p.keyof(p.yo(Y - dy), p.xo(X - dx), p.c)
                    for b in range(half):
                        at = (t * half + b) * BLOCK_COLUMNS + key * piece
                        dst = w.at[pl.ds(pl.multiple_of(at, 16), piece)]
                        i = ((t * Y + dy) * X + dx) * half + b
                        wcopies.append(pltpu.make_async_copy(src.at[b], dst, wsem.at[i]))
                        wremote.append(remote(src.at[b], dst, wsend.at[i], wrecv.at[i], p.core_peer()))
    else:
        wcopies.append(pltpu.make_async_copy(w_refs[0], w, wsem.at[0]))
    for copy in wcopies:
        copy.start()
    p.meet()

    n = sems_per_item(Y, X) * 2
    merges = []
    for m in range(micro):
        for g in range(groups):
            i = m * groups + g
            item = Scatter(
                p,
                [o_ref.at[m, :, :, :, pl.ds(g * rows, rows)], st_ref.at[m, g]],
                [oa.at[i], sa.at[i]], [o1.at[i], s1.at[i]], [o2.at[i], s2.at[i]], [o3.at[i], s3.at[i]],
                send, recv, loc, i * n, i * 2, g % 2 == 0, merge_soft,
            )
            merges.append(item)

    def merge_one(m):
        for g in range(groups):
            merges[m * groups + g].start1()

    def merge_two(m):
        for g in range(groups):
            merges[m * groups + g].start2()

    def merge_three(m):
        for g in range(groups):
            merges[m * groups + g].start3()

    def merge_finish(m):
        for g in range(groups):
            val, st = merges[m * groups + g].finish()
            tile = st[...]
            inv = 1.0 / tile[GROUP:]
            stat[m, g, :GROUP] = tile[:GROUP]
            invs_ref[m, g] = inv
            for h in range(GROUP):
                att[m, g * rows + h * HD : g * rows + (h + 1) * HD, :] = (
                    val[h * HD : (h + 1) * HD, :].astype(F32) * inv[h : h + 1]
                ).astype(BF16)

    n = sems_per_item(Y, X)
    gathers = [[], []]
    for m in range(micro):
        for g in range(groups):
            ds = pl.ds(g * rows, rows)
            for t, (own, out) in enumerate(
                ((datt.at[m, ds], datt_out.at[m, :, :, :, ds]), (stat.at[m, g], stat_out.at[m, g]))
            ):
                i = (m * groups + g) * 2 + t
                gathers[m].append(
                    (
                        Gather(p, own, out, gsend, grecv, i * n, g % 2 == 0),
                        pltpu.make_async_copy(own, out.at[p.y, p.x, p.c], gloc.at[i]),
                    )
                )

    def gather_one(m):
        for item, copy in gathers[m]:
            item.start1()
            copy.start()

    def gather_two(m):
        for item, copy in gathers[m]:
            copy.wait()
            item.start2()

    def gather_three(m):
        for item, copy in gathers[m]:
            item.start3()

    def forward(m):
        at = att[m].T
        attk[m] = at
        wo = w[:width]
        z1 = x_ref[m].astype(F32) + (dot_f32(at, wo, ((1,), (1,))) + bo)
        norm, inv = layer_norm(z1)
        n1[...] = norm
        mid = norm * g1 + e1
        low[m] = mid.astype(BF16)
        inner = low[m]

        def body(i, acc):
            r = pl.multiple_of(i * wide, wide)
            pre = dot_f32(inner, w[pl.ds(width + r, wide)], ((1,), (1,))) + bu_ref[:, pl.ds(r, wide)]
            half = 0.5 + 0.5 * lax.erf(pre * math.sqrt(0.5))
            low_h = (pre * half).astype(BF16)
            hid[m, :, pl.ds(r, wide)] = low_h
            slope[:, pl.ds(r, wide)] = half + pre * (
                jnp.exp(-0.5 * pre * pre) * (1.0 / math.sqrt(2.0 * math.pi))
            )
            return acc + dot_f32(low_h, w[pl.ds(width + FF + r, wide)], ((1,), (0,)))

        f = lax.fori_loop(0, parts, body, jnp.zeros((tok, width), F32)) + bd
        norm2, inv2 = layer_norm(mid + f)
        n2[...] = norm2
        out_ref[m] = (norm2 * g2 + e2).astype(BF16)
        return inv, inv2

    def backward(m, invs, between=lambda: None):
        inv, inv2 = invs
        cot = cot_ref[m].astype(F32)
        norm2 = n2[...]
        dz2 = norm_back(cot, norm2, inv2, g2)
        dg2 = jnp.sum(cot * norm2, axis=0, keepdims=True)
        de2 = jnp.sum(cot, axis=0, keepdims=True)
        df_low = dz2.astype(BF16)
        df[m] = df_low
        dbd = jnp.sum(df_low.astype(F32), axis=0, keepdims=True)

        def body(i, acc):
            r = pl.multiple_of(i * wide, wide)
            dh = dot_f32(df_low, w[pl.ds(width + FF + r, wide)], ((1,), (1,)))
            dp = (dh * slope[:, pl.ds(r, wide)]).astype(BF16)
            dpre[m, :, pl.ds(r, wide)] = dp
            part = jnp.sum(dp.astype(F32), axis=0, keepdims=True)
            dbu_ref[:, pl.ds(r, wide)] += part
            return acc + dot_f32(dp, w[pl.ds(width + r, wide)], ((1,), (0,)))

        dx1 = lax.fori_loop(0, parts // 2, body, dz2)
        between()
        dx1 = lax.fori_loop(parts // 2, parts, body, dx1)
        norm = n1[...]
        dg1 = jnp.sum(dx1 * norm, axis=0, keepdims=True)
        de1 = jnp.sum(dx1, axis=0, keepdims=True)
        dz1 = norm_back(dx1, norm, inv, g1)
        dz_ref[m] = dz1
        da_low = dz1.astype(BF16)
        da[m] = da_low
        dbo = jnp.sum(da_low.astype(F32), axis=0, keepdims=True)
        sums = jnp.concatenate([dbo, dg1, de1, dbd, dg2, de2, dg2, dg2], axis=0)
        dvec_ref[...] += sums
        dt = dot_f32(da_low, w[:width], ((1,), (0,))).T
        for g in range(groups):
            for h in range(GROUP):
                r = g * rows + h * HD
                part = dt[r : r + HD] * invs_ref[m, g, h : h + 1]
                datt[m, r : r + HD, :] = part.astype(BF16)
                stat[m, g, GROUP + h : GROUP + h + 1] = jnp.sum(
                    part * att[m, r : r + HD, :].astype(F32), axis=0, keepdims=True
                )

    step = width // 2

    def chunk_grad(slot, at, chunk):
        for left, right, lo, count in ((da, attk, 0, width), (dpre, low, width, FF), (hid, df, width + FF, FF)):

            @pl.when((chunk * step >= lo) & (chunk * step < lo + count))
            def _():
                cols = pl.ds(pl.multiple_of(chunk * step - lo, step), step)
                total = dot_f32(left[0, :, cols], right[0], ((0,), (0,)))
                for m in range(1, micro):
                    total = total + dot_f32(left[m, :, cols], right[m], ((0,), (0,)))
                dw[slot, pl.ds(pl.multiple_of(at, step), step)] = total.astype(BF16)

    def block_grad(b, slot):
        per = BLOCK_COLUMNS // step

        def body(t, carry):
            chunk_grad(slot, t * step, b * per + t)
            return carry

        lax.fori_loop(0, per, body, 0)

    merge_one(0)
    merge_two(0)
    for copy in wremote:
        copy.start()
    merge_one(1)
    merge_three(0)
    merge_two(1)
    merge_finish(0)
    for copy in wcopies:
        copy.wait()
    for copy in wremote:
        copy.wait_recv()
    dvec_ref[...] = jnp.zeros_like(dvec_ref)
    dbu_ref[...] = jnp.zeros_like(dbu_ref)

    def turn(m, carry):
        invs = forward(m)
        pl.when(m == 1)(lambda: gather_two(0))
        backward(m, invs, lambda: pl.when(m == 0)(lambda: merge_three(1)))

        @pl.when(m == 0)
        def _():
            gather_one(0)
            merge_finish(1)

        @pl.when(m == 1)
        def _():
            gather_one(1)
            gather_three(0)

        return carry

    lax.fori_loop(0, micro, turn, 0)
    if pieces:
        half, piece = w_refs[0].shape[:2]
        keeps = []

        def cores(b):
            slot = lax.rem(b, 2)
            copies = []
            for y in range(Y):
                for x in range(X):
                    i = (b * Y + y) * X + x
                    there = pl.multiple_of(p.keyof(y, x, 1 - p.c) * piece, 16)
                    copies.append(
                        remote(
                            dw.at[slot, pl.ds(there, piece)], core_in.at[b, y, x],
                            csend.at[i], crecv.at[i], p.core_peer(),
                        )
                    )
            return copies

        def one_block(b, carry):
            slot = lax.rem(b, 2)

            @pl.when(b >= 2)
            def _():
                for copy in cores(b - 2):
                    copy.wait_send()

            block_grad(b, slot)
            for copy in cores(b):
                copy.start()
            for y in range(Y):
                for x in range(X):
                    here = pl.multiple_of(p.keyof(y, x, p.c) * piece, 16)
                    core_acc[b, y, x] = dw[slot, pl.ds(here, piece)]
            return carry

        lax.fori_loop(0, blocks // 2, one_block, 0)
        gather_two(1)
        lax.fori_loop(blocks // 2, blocks, one_block, 0)
        gather_three(1)

        def add(i, carry):
            b, y, x = i // (Y * X), lax.rem(i // X, Y), lax.rem(i, X)
            merge_sum([core_acc.at[b, y, x]], [core_in.at[b, y, x]])
            return carry

        def add_block(b, carry):
            for copy in cores(b):
                copy.wait_recv()
            lax.fori_loop(b * Y * X, (b + 1) * Y * X, add, 0)
            return carry

        lax.fori_loop(0, blocks, add_block, 0)
        first, last = pl.ds(0, half), pl.ds(half, half)
        for x in range(X):
            keeps.append((core_acc.at[first, p.y, x], keep_a.at[x]))
            for d in range(1, Y):
                keeps.append((core_acc.at[first, p.yo(d), x], send_a.at[d - 1, x]))
        for y in range(Y):
            keeps.append((core_acc.at[last, y, p.x], keep_b.at[y]))
            for d in range(1, X):
                keeps.append((core_acc.at[last, y, p.xo(d)], send_b.at[d - 1, y]))
        keeps = [pltpu.make_async_copy(src, dst, dwsem.at[i]) for i, (src, dst) in enumerate(keeps)]
        for copy in keeps:
            copy.start()
        for copy in keeps:
            copy.wait()
        for b in (blocks - 2, blocks - 1):
            for copy in cores(jnp.int32(b)):
                copy.wait_send()
    else:
        copies = []
        for b in range(blocks):
            slot = b % 2
            if b >= 2:
                copies[b - 2].wait()
            block_grad(b, slot)
            copies.append(
                pltpu.make_async_copy(
                    dw.at[slot], dw_out.at[pl.ds(b * BLOCK_COLUMNS, BLOCK_COLUMNS)], dwsem.at[slot]
                )
            )
            copies[-1].start()
            if b == blocks // 2:
                gather_two(1)
        for copy in copies[-2:]:
            copy.wait()
        gather_three(1)
    for item in merges:
        item.drain()
    for copy in wremote:
        copy.wait_send()
    for m in range(micro):
        for item, copy in gathers[m]:
            item.finish()


def middle(mesh_dims, o_part, st_part, x_own, cot, weights, vec, bias_up):
    Y, X, R = mesh_dims
    micro, tok, width = x_own.shape
    groups = st_part.shape[1]
    items = micro * groups
    merge_sems = sems_per_item(Y, X) * 2 * items
    strows = STAT_ROWS
    ffw = 2 * FF + width
    blocks = ffw // BLOCK_COLUMNS
    pieces = len(weights) > 1
    outs = [
        (jax.ShapeDtypeStruct((micro, tok, width), BF16), VMEM_SPEC),
        (jax.ShapeDtypeStruct((micro, Y, X, 2, width, tok), BF16), ANY),
        (jax.ShapeDtypeStruct((micro, groups, Y, X, 2, strows, tok), F32), ANY),
        (jax.ShapeDtypeStruct((micro, tok, width), F32), VMEM_SPEC),
        (jax.ShapeDtypeStruct((8, width), F32), VMEM_SPEC),
        (jax.ShapeDtypeStruct((1, FF), F32), VMEM_SPEC),
    ]
    extra = []
    if pieces:
        half, piece = weights[0].shape[:2]
        wsems = 2 * Y * X * half
        outs += [
            (jax.ShapeDtypeStruct((max(Y - 1, 1), X, half, piece, width), BF16), ANY),
            (jax.ShapeDtypeStruct((X, half, piece, width), BF16), ANY),
            (jax.ShapeDtypeStruct((max(X - 1, 1), Y, half, piece, width), BF16), ANY),
            (jax.ShapeDtypeStruct((Y, half, piece, width), BF16), ANY),
        ]
        extra = [
            pltpu.VMEM((blocks, Y, X, piece, width), BF16),
            pltpu.VMEM((blocks, Y, X, piece, width), BF16),
            pltpu.SemaphoreType.DMA((blocks * Y * X,)),
            pltpu.SemaphoreType.DMA((blocks * Y * X,)),
        ]
    else:
        wsems = 1
        outs += [(jax.ShapeDtypeStruct((ffw, width), BF16), ANY)]
    return pl.pallas_call(
        functools.partial(middle_kernel, Y, X, R, blocks, pieces),
        out_shape=tuple(o for o, _ in outs),
        in_specs=[ANY, ANY, VMEM_SPEC, VMEM_SPEC, VMEM_SPEC, VMEM_SPEC] + [ANY] * len(weights),
        out_specs=tuple(spec for _, spec in outs),
        scratch_shapes=scatter_scratch(Y, X, items, (GROUP * HD, tok), BF16, None)
        + scatter_scratch(Y, X, items, (2 * GROUP, tok), F32, None)
        + [
            pltpu.SemaphoreType.DMA((merge_sems,)),
            pltpu.SemaphoreType.DMA((merge_sems,)),
            pltpu.SemaphoreType.DMA((items * 2,)),
            pltpu.SemaphoreType.DMA((merge_sems,)),
            pltpu.SemaphoreType.DMA((merge_sems,)),
            pltpu.SemaphoreType.DMA((items * 2,)),
            pltpu.SemaphoreType.DMA((wsems,)),
            pltpu.SemaphoreType.DMA((wsems,)),
            pltpu.SemaphoreType.DMA((wsems,)),
            pltpu.SemaphoreType.DMA((2 * X * Y,)),
            pltpu.VMEM((ffw, width), BF16),
            pltpu.VMEM((micro, width, tok), BF16),
            pltpu.VMEM((micro, tok, width), BF16),
            pltpu.VMEM((micro, tok, width), BF16),
            pltpu.VMEM((micro, tok, FF), BF16),
            pltpu.VMEM((micro, tok, FF), BF16),
            pltpu.VMEM((tok, FF), F32),
            pltpu.VMEM((micro, tok, width), BF16),
            pltpu.VMEM((micro, tok, width), BF16),
            pltpu.VMEM((tok, width), F32),
            pltpu.VMEM((tok, width), F32),
            pltpu.VMEM((micro, width, tok), BF16),
            pltpu.VMEM((micro, groups, strows, tok), F32),
            pltpu.VMEM((micro, groups, GROUP, tok), F32),
            pltpu.VMEM((2, BLOCK_COLUMNS, width), BF16),
        ]
        + extra,
        compiler_params=pltpu.CompilerParams(
            collective_id=2, has_side_effects=True, vmem_limit_bytes=VMEM_LIMIT
        ),
        name="middle",
    )(o_part, st_part, x_own, cot, vec, bias_up, *weights)


def tail_kernel(
    Y, X, R, inverse,
    dq_ref, dk_hbm, dv_hbm, x_hbm, dz_hbm, w_ref, vec_ref, bu_ref, xg_ref, dqs_hbm, *refs,
):
    suma_hbm, got_a, sumb_hbm, got_b = refs[0], refs[1:X], refs[X], refs[X + 1 : X + Y]
    tok_ref, late_ref, early_ref, sum_ref = refs[X + Y : X + Y + 4]
    (
        qa, q1, q2, q3, send, recv, loc,
        part, a, r1, r2, r3, bsend, brecv, bloc,
        fin, stage, rz, zsend, zrecv, qf, qz, rq, qsend, qrecv,
        small, sbuf, ssend, srecv, w, wsem, dq, dqv, xv, acc, vsem,
        dk_ref, dv_ref, x_ref, dqs_ref, sum_a, sum_b, dz_ref, fsem,
    ) = refs[X + Y + 4 :]
    p = Place(Y, X, R)
    micro, tok, width = x_ref.shape
    slots_here = late_ref.shape[0]
    groups = qa.shape[0] // micro
    rows = GROUP * HD
    n = sems_per_item(Y, X)
    piece = part.shape[4]
    p.announce(True)
    outer = (dk_hbm, dv_hbm, x_hbm, dqs_hbm, suma_hbm, sumb_hbm, dz_hbm)
    inner = (dk_ref, dv_ref, x_ref, dqs_ref, sum_a, sum_b, dz_ref)
    fetch = [pltpu.make_async_copy(a, b, fsem.at[i]) for i, (a, b) in enumerate(zip(outer, inner))]
    loads = [
        pltpu.make_async_copy(dq_ref, dqv, vsem.at[0]),
        pltpu.make_async_copy(xg_ref, xv, vsem.at[1]),
    ]
    wcopy = pltpu.make_async_copy(w_ref, w, wsem)
    for copy in fetch + loads + [wcopy]:
        copy.start()
    for copy in fetch[:6]:
        copy.wait()
    for at, total, got in ((p.x, sum_a, got_a), (p.y, sum_b, got_b)):
        count = total.shape[1]
        base = 0 if total is sum_a else count

        def add(b, carry, at=at, total=total, got=got, base=base):
            value = total[at, b].astype(F32)
            for ref in got:
                value = value + ref[b].astype(F32)
            fin[base + b] = value.astype(BF16)
            return carry

        lax.fori_loop(0, count, add, 0)

    def reorder(s, carry):
        stage[s] = fin[jnp.maximum(inverse[s] - EARLY, 0)]
        return carry

    lax.fori_loop(0, stage.shape[0], reorder, 0)
    ones = jnp.ones((8, tok), BF16)
    bias_v = dot_f32(ones, dv_ref[0], ((1,), (1,)))
    sum_q = dqs_ref[0]
    for m in range(1, micro):
        bias_v = bias_v + dot_f32(ones, dv_ref[m], ((1,), (1,)))
        sum_q = sum_q + dqs_ref[m]
    sums = [sum_q.T[:1], bias_v[:1], vec_ref[:3]]
    sums += [bu_ref[:, i * width : (i + 1) * width] for i in range(FF // width)]
    sums += [vec_ref[3:6], jnp.zeros((4, width), F32)]
    small[...] = jnp.concatenate(sums, axis=0).astype(BF16)
    stages = [[p.core_peer()]]
    stages.append([p.x_peer(d) for d in range(1, X)])
    stages.append([p.y_peer(d) for d in range(1, Y)])
    stages.append([p.z_peer(d) for d in range(1, R)])
    scopies = []
    at = 0
    for peers in stages:
        row = []
        for peer in peers:
            row.append(remote(small, sbuf.at[at], ssend.at[at], srecv.at[at], peer))
            at += 1
        scopies.append(row)

    def small_start(t):
        for copy in scopies[t]:
            copy.start()

    def small_wait(t):
        at = sum(len(row) for row in scopies[:t])
        for copy in scopies[t]:
            copy.wait_recv()
        for copy in scopies[t]:
            copy.wait_send()
        total = small[...].astype(F32)
        for i in range(len(scopies[t])):
            total = total + sbuf[at + i].astype(F32)
        return total

    def token_grad(m):
        total = dz_ref[m] + dot_f32(dq[m], w[:width], ((0,), (0,)))
        total = total + dot_f32(dk_ref[m], w[width : 2 * width], ((0,), (0,)))
        total = total + dot_f32(dv_ref[m], w[2 * width :], ((0,), (0,)))
        tok_ref[m] = total.astype(BF16)

    p.meet()
    small_start(0)
    zcopies = []
    if R == 4:
        near = p.r + 1 - 2 * lax.rem(p.r, 2)
        far = p.ro(2)
        classes = (p.r, far)
        one = [
            [
                remote(
                    stage.at[q * slots_here + s], rz.at[k, s], zsend.at[k, s], zrecv.at[k, s], {"rows": near}
                )
                for k, q in enumerate((near, lax.rem(near + 2, R)))
            ]
            for s in range(slots_here)
        ]
        two = [
            remote(stage.at[far * slots_here + s], rz.at[2, s], zsend.at[2, s], zrecv.at[2, s], {"rows": far})
            for s in range(slots_here)
        ]
        for copies in one:
            for copy in copies:
                copy.start()

        def z_pass(s):
            for copy in one[s]:
                copy.wait_recv()
            for k, q in enumerate(classes):
                merge_sum([stage.at[q * slots_here + s]], [rz.at[k, s]])
            two[s].start()

        def z_total(s):
            two[s].wait_recv()
            return stage[p.r * slots_here + s].astype(F32) + rz[2, s].astype(F32)

        zcopies = [copy for copies in one for copy in copies] + two
    else:
        for d in range(1, R):
            there = pl.ds(p.ro(d) * slots_here, slots_here)
            copy = remote(stage.at[there], rz.at[d - 1], zsend.at[d - 1, 0], zrecv.at[d - 1, 0], p.z_peer(d))
            copy.start()
            zcopies.append(copy)

        def z_pass(s):
            pass

        def z_total(s):
            if s == 0:
                for copy in zcopies:
                    copy.wait_recv()
            total = stage[p.r * slots_here + s].astype(F32)
            for d in range(1, R):
                total = total + rz[d - 1, s].astype(F32)
            return total

    qitems = []
    for m in range(micro):
        for g in range(groups):
            i = m * groups + g
            item = Scatter(
                p, [dq_ref.at[m, :, :, :, pl.ds(g * rows, rows)]],
                [qa.at[i]], [q1.at[i]], [q2.at[i]], [q3.at[i]],
                send, recv, loc, i * n, i, g % 2 == 0, merge_sum,
            )
            qitems.append(item)
    first, last = qitems[: len(qitems) - groups], qitems[len(qitems) - groups :]
    for item in first:
        item.start1()

    def product(ref, first, count):
        total = dot_f32(ref[0, first : first + count], x_ref[0], ((1,), (0,)))
        for m in range(1, micro):
            total = total + dot_f32(ref[m, first : first + count], x_ref[m], ((1,), (0,)))
        return total.astype(BF16)

    def put(b, first, value):
        at = 0
        while at < value.shape[0]:
            key, off = divmod(first + at, piece)
            count = min(piece - off, value.shape[0] - at)
            y, x, c = key // (2 * X), key // 2 % X, key % 2
            part[b, y, x, c, off : off + count] = value[at : at + count]
            at += count

    cuts = ((0, piece // 32 * 16, True), (piece // 32 * 16, piece - piece // 32 * 16, False))

    def block_items(b):
        out = []
        for t, (first, count, y_first) in enumerate(cuts):
            ds = pl.ds(first, count)
            i = b * len(cuts) + t
            out.append(
                Scatter(
                    p, [part.at[b, :, :, :, ds]], [a.at[b, :, :, ds]], [r1.at[b, :, :, ds]],
                    [r2.at[b, :, :, ds]], [r3.at[b, :, ds]],
                    bsend, brecv, bloc, i * n, i, y_first, merge_sum,
                )
            )
        return out

    class Block:
        def __init__(self, b):
            self.b, self.items = b, block_items(b)
            self.one = [
                remote(qz.at[b, p.ro(d)], rq.at[b, d - 1], qsend.at[b, 0, d], qrecv.at[b, 0, d], p.z_peer(d))
                for d in range(1, R)
            ]
            mine = early_ref.at[b, p.r]
            self.two = [
                remote(mine, mine, qsend.at[b, 1, d], qrecv.at[b, 1, d], p.z_peer(d)) for d in range(1, R)
            ]

        def step(self, name):
            for item in self.items:
                getattr(item, name)()

        def z_one(self):
            for item, (first, count, _) in zip(self.items, cuts):
                (val,) = item.finish()
                qf[first : first + count] = val[...].astype(F32)
            share = qz.shape[2]
            for i in range(R):
                qz[self.b, i] = qf[i * share : (i + 1) * share].astype(BF16)
            for copy in self.one:
                copy.start()

        def z_two(self):
            for copy in self.one:
                copy.wait_recv()
            total = qz[self.b, p.r].astype(F32)
            for d in range(1, R):
                total = total + rq[self.b, d - 1].astype(F32)
            early_ref[self.b, p.r] = total.astype(BF16)
            for copy in self.two:
                copy.start()

        def finish(self):
            for copy in self.two:
                copy.wait_recv()
            for item in self.items:
                item.drain()
            for copy in self.one + self.two:
                copy.wait_send()

    block0, block1 = Block(0), Block(1)
    half = width // 2
    put(1, 0, product(dk_ref, half, half))
    small[...] = small_wait(0).astype(BF16)
    small_start(1)
    put(1, half, product(dv_ref, 0, width))
    block1.step("start1")
    small[...] = small_wait(1).astype(BF16)
    small_start(2)
    put(0, width, product(dk_ref, 0, half))
    small[...] = small_wait(2).astype(BF16)
    small_start(3)
    for item in first:
        item.start2()
    for item in last:
        item.start1()
    for copy in loads:
        copy.wait()
    acc[...] = jnp.zeros_like(acc)
    line = 2 * tok
    turns = micro * Y * X

    def query_grad(i, carry):
        m, y, x = i // (Y * X), lax.rem(i // X, Y), lax.rem(i, X)
        left = jnp.concatenate([dqv[m, y, x, c] for c in range(2)], axis=1)
        right = xv[m, pl.ds(pl.multiple_of(lax.rem(i, Y * X) * line, line), line)]
        acc[...] += dot_f32(left, right, ((1,), (0,)))
        return carry

    lax.fori_loop(0, turns // 2, query_grad, 0)
    z_pass(0)
    lax.fori_loop(turns // 2, turns, query_grad, 0)
    put(0, 0, acc[...].astype(BF16))
    block0.step("start1")
    block1.step("start2")
    block0.step("start2")
    for s in range(1, slots_here):
        z_pass(s)
    block1.step("start3")
    block0.step("start3")
    for item in last:
        item.start2()
    for item in first:
        item.start3()
    block1.z_one()
    block0.z_one()
    for item in last:
        item.start3()
    block1.z_two()
    block0.z_two()
    for s in range(slots_here):
        late_ref[s] = z_total(s)
    wcopy.wait()
    fetch[6].wait()
    def token_grad(m, carry):
        for k in range(micro):

            @pl.when(m == k)
            def _():
                for g in range(groups):
                    (val,) = qitems[k * groups + g].finish()
                    dq[k, g * rows : (g + 1) * rows, :] = val[...]

        total = dz_ref[m] + dot_f32(dq[m], w[:width], ((0,), (0,)))
        total = total + dot_f32(dk_ref[m], w[width : 2 * width], ((0,), (0,)))
        total = total + dot_f32(dv_ref[m], w[2 * width :], ((0,), (0,)))
        tok_ref[m] = total.astype(BF16)
        return carry

    lax.fori_loop(0, micro, token_grad, 0)
    sum_ref[...] = small_wait(3)
    block1.finish()
    block0.finish()
    for item in qitems:
        item.drain()
    for copy in zcopies:
        copy.wait_send()


def tail(mesh_dims, inverse, dq_part, dk, dv, x_own, grad_one, w_early, fin_a, fin_b, dvec, d_bias_up, x_all, dq_sum):
    Y, X, R = mesh_dims
    micro, tok, width = x_own.shape
    half, n = fin_a[0].shape[1:3]
    late = 2 * half
    blocks = EARLY + late
    slots_here = blocks // R
    groups = width // (GROUP * HD)
    items = micro * groups
    per = sems_per_item(Y, X)
    share = n // R
    cuts = 2
    small = (16, width)
    hops = 1 + (X - 1) + (Y - 1) + (R - 1)
    return pl.pallas_call(
        functools.partial(tail_kernel, Y, X, R),
        out_shape=(
            jax.ShapeDtypeStruct((micro, tok, width), BF16),
            jax.ShapeDtypeStruct((slots_here, n, width), F32),
            jax.ShapeDtypeStruct((EARLY, R, share, width), BF16),
            jax.ShapeDtypeStruct(small, F32),
        ),
        in_specs=[pl.BlockSpec(memory_space=pltpu.SMEM), ANY]
        + [ANY] * 4
        + [ANY, VMEM_SPEC, VMEM_SPEC, ANY, ANY]
        + ([ANY] + [VMEM_SPEC] * (X - 1) + [ANY] + [VMEM_SPEC] * (Y - 1)),
        out_specs=(VMEM_SPEC,) * 4,
        scratch_shapes=scatter_scratch(Y, X, items, (GROUP * HD, tok), BF16, None)
        + [
            pltpu.SemaphoreType.DMA((per * items,)),
            pltpu.SemaphoreType.DMA((per * items,)),
            pltpu.SemaphoreType.DMA((items,)),
            pltpu.VMEM((EARLY, Y, X, 2, n, width), BF16),
        ]
        + scatter_scratch(Y, X, EARLY, (n, width), BF16, None)
        + [
            pltpu.SemaphoreType.DMA((per * EARLY * cuts,)),
            pltpu.SemaphoreType.DMA((per * EARLY * cuts,)),
            pltpu.SemaphoreType.DMA((EARLY * cuts,)),
            pltpu.VMEM((late, n, width), BF16),
            pltpu.VMEM((blocks, n, width), BF16),
            pltpu.VMEM((R - 1, slots_here, n, width), BF16),
            pltpu.SemaphoreType.DMA((R - 1, slots_here)),
            pltpu.SemaphoreType.DMA((R - 1, slots_here)),
            pltpu.VMEM((n, width), F32),
            pltpu.VMEM((EARLY, R, share, width), BF16),
            pltpu.VMEM((EARLY, R - 1, share, width), BF16),
            pltpu.SemaphoreType.DMA((EARLY, 2, R)),
            pltpu.SemaphoreType.DMA((EARLY, 2, R)),
            pltpu.VMEM(small, BF16),
            pltpu.VMEM((hops,) + small, BF16),
            pltpu.SemaphoreType.DMA((hops,)),
            pltpu.SemaphoreType.DMA((hops,)),
            pltpu.VMEM((3 * width, width), BF16),
            pltpu.SemaphoreType.DMA,
            pltpu.VMEM((micro, width, tok), BF16),
            pltpu.VMEM(dq_part.shape, BF16),
            pltpu.VMEM(x_all.shape, BF16),
            pltpu.VMEM((width, width), F32),
            pltpu.SemaphoreType.DMA((2,)),
            pltpu.VMEM(dk.shape, BF16),
            pltpu.VMEM(dv.shape, BF16),
            pltpu.VMEM(x_own.shape, BF16),
            pltpu.VMEM(dq_sum.shape, F32),
            pltpu.VMEM(fin_a[0].shape, BF16),
            pltpu.VMEM(fin_b[0].shape, BF16),
            pltpu.VMEM(grad_one.shape, F32),
            pltpu.SemaphoreType.DMA((7,)),
        ],
        compiler_params=pltpu.CompilerParams(
            collective_id=5, has_side_effects=True, vmem_limit_bytes=VMEM_LIMIT
        ),
        name="tail",
    )(inverse, dq_part, dk, dv, x_own, grad_one, w_early.reshape(3 * width, width), dvec, d_bias_up, x_all, dq_sum, *fin_a, *fin_b)


def project_kernel(scale, x_ref, own_ref, w_ref, vec_ref, q_ref, k_ref, v_ref, bias):
    width = x_ref.shape[2]

    @pl.when((pl.program_id(0) == 0) & (pl.program_id(1) == 0))
    def _():
        bias[...] = vec_ref[...].T

    q = dot_f32(w_ref[:width], x_ref[0], ((1,), (1,))) + bias[:, 6:7]
    q_ref[0] = q.astype(BF16) * jnp.asarray(scale, BF16)

    @pl.when(pl.program_id(1) == 0)
    def _():
        own = own_ref[0]
        k_ref[0] = dot_f32(w_ref[width : 2 * width], own, ((1,), (1,))).astype(BF16)
        v_ref[0] = (dot_f32(w_ref[2 * width :], own, ((1,), (1,))) + bias[:, 7:8]).astype(BF16)


def project(x_all, x_own, w_t, vec, scale):
    micro, slots, width = x_all.shape
    own = x_own.shape[1]
    wide = min(1024, slots)
    return pl.pallas_call(
        functools.partial(project_kernel, scale),
        grid=(micro, slots // wide),
        out_shape=(
            jax.ShapeDtypeStruct((micro, width, slots), BF16),
            jax.ShapeDtypeStruct((micro, width, own), BF16),
            jax.ShapeDtypeStruct((micro, width, own), BF16),
        ),
        in_specs=[
            pl.BlockSpec((1, wide, width), lambda m, t: (m, t, 0)),
            pl.BlockSpec((1, own, width), lambda m, t: (m, 0, 0)),
            pl.BlockSpec((3 * width, width), lambda m, t: (0, 0)),
            pl.BlockSpec((8, width), lambda m, t: (0, 0)),
        ],
        out_specs=(
            pl.BlockSpec((1, width, wide), lambda m, t: (m, 0, t)),
            pl.BlockSpec((1, width, own), lambda m, t: (m, 0, 0)),
            pl.BlockSpec((1, width, own), lambda m, t: (m, 0, 0)),
        ),
        scratch_shapes=[pltpu.VMEM((width, 8), F32)],
        compiler_params=pltpu.CompilerParams(vmem_limit_bytes=VMEM_LIMIT),
        cost_estimate=pl.CostEstimate(
            flops=2 * micro * width * width * (slots + 2 * own),
            bytes_accessed=4 * micro * width * slots,
            transcendentals=0,
        ),
        name="project",
    )(x_all, x_own, w_t, vec)


def attention_forward_kernel(q_ref, k_ref, v_ref, prev_ref, segk_ref, segq_ref, *refs):
    logit_ref, e_ref, o_ref, st_ref, top_ref, mask_ref = refs[-6:]
    h = pl.program_id(0)
    chunks, wide = o_ref.shape[1], o_ref.shape[3]

    @pl.when(h == 0)
    def _():
        mask_ref[...] = jnp.where(segk_ref[0] == segq_ref[0], 0.0, NEG_BIG)

    for i in range(PER):
        rows = slice(i * HD, (i + 1) * HD)
        hg = lax.rem(h * PER + i, GROUP)
        score = dot_f32(k_ref[rows], q_ref[rows], ((0,), (0,)))
        raw = score + prev_ref[0, 0, i].astype(F32)
        logit_ref[0, 0, i] = raw.astype(BF16)
        masked = raw + mask_ref[...]
        top = jnp.maximum(jnp.max(masked, axis=0, keepdims=True), NEG_FLOOR)
        expo = jnp.exp(masked - top)
        total = jnp.sum(expo, axis=0, keepdims=True)
        low = expo.astype(BF16)
        e_ref[0, i] = low
        out = dot_f32(v_ref[rows], low, ((1,), (0,))).astype(BF16)
        for t in range(chunks):
            cols = slice(t * wide, (t + 1) * wide)
            o_ref[0, t, rows] = out[:, cols]
            st_ref[0, 0, t, pl.ds(hg, 1), :] = top[:, cols]
            st_ref[0, 0, t, pl.ds(GROUP + hg, 1), :] = total[:, cols]
            top_ref[0, 0, t, pl.ds(hg, 1), :] = top[:, cols]


def attention_forward(m, so_far, q, k, v, prev, segk, segq, chunks, wide):
    micro, _, heads, own, slots = prev.shape
    groups = heads // GROUP
    score = pl.BlockSpec((1, 1, PER, own, slots), lambda h: (m, 0, h, 0, 0))
    stat = pl.BlockSpec((1, 1, chunks, 2 * GROUP, wide), lambda h: (m, h * PER // GROUP, 0, 0, 0))
    return pl.pallas_call(
        attention_forward_kernel,
        grid=(heads // PER,),
        out_shape=(
            jax.ShapeDtypeStruct(prev.shape, BF16),
            jax.ShapeDtypeStruct((micro, heads, own, slots), BF16),
            jax.ShapeDtypeStruct((micro, chunks, heads * HD, wide), BF16),
            jax.ShapeDtypeStruct((micro, groups, chunks, 2 * GROUP, wide), F32),
            jax.ShapeDtypeStruct((micro, groups, chunks, 2 * GROUP, wide), F32),
        ),
        in_specs=[
            pl.BlockSpec((None, PER * HD, slots), lambda h: (m, h, 0)),
            pl.BlockSpec((None, PER * HD, own), lambda h: (m, h, 0)),
            pl.BlockSpec((None, PER * HD, own), lambda h: (m, h, 0)),
            score,
            pl.BlockSpec((1, own, 1), lambda h: (m, 0, 0)),
            pl.BlockSpec((1, 1, slots), lambda h: (m, 0, 0)),
        ]
        + [ANY] * len(so_far),
        out_specs=(
            score,
            pl.BlockSpec((1, PER, own, slots), lambda h: (m, h, 0, 0)),
            pl.BlockSpec((1, chunks, PER * HD, wide), lambda h: (m, 0, h, 0)),
            stat,
            stat,
        ),
        input_output_aliases={6 + i: i for i in range(len(so_far))},
        scratch_shapes=[pltpu.VMEM((own, slots), F32)],
        compiler_params=pltpu.CompilerParams(vmem_limit_bytes=VMEM_LIMIT),
        cost_estimate=pl.CostEstimate(
            flops=heads * 2 * 2 * own * slots * HD,
            bytes_accessed=heads * own * slots * 6,
            transcendentals=heads * own * slots,
        ),
        name="attention_forward",
    )(q, k, v, prev, segk, segq, *so_far)


def attention_backward_kernel(
    scale, first, e_ref, d_ref, st_ref, top_ref, q_ref, k_ref, v_ref, *refs
):
    g_ref, dq_ref, dk_ref, dv_ref, sum_ref = refs[-5:]
    h = pl.program_id(0) + first
    chunks, wide = d_ref.shape[1], d_ref.shape[3]
    for i in range(PER):
        rows = slice(i * HD, (i + 1) * HD)
        hg = lax.rem(h * PER + i, GROUP)

        def row(ref, first):
            return jnp.concatenate([ref[0, 0, t, pl.ds(first + hg, 1), :] for t in range(chunks)], axis=1)

        weight = jnp.exp(row(top_ref, 0) - row(st_ref, 0))
        dots = row(st_ref, GROUP) * weight
        low = e_ref[0, i]
        datt = jnp.concatenate([d_ref[0, t, rows] for t in range(chunks)], axis=1)
        grad_in = (datt.astype(F32) * weight).astype(BF16)
        soft = dot_f32(v_ref[rows], grad_in, ((0,), (0,))) - dots
        grad = (low.astype(F32) * soft).astype(BF16)
        g_ref[0, 0, i] = grad
        dq = dot_f32(k_ref[rows], grad, ((1,), (0,))) * scale
        sum_ref[0, rows] = jnp.broadcast_to(jnp.sum(dq, axis=1, keepdims=True), (HD, 128))
        dq = dq.astype(BF16)
        for t in range(chunks):
            dq_ref[0, t, rows] = dq[:, t * wide : (t + 1) * wide]
        dv_ref[0, rows] = dot_f32(grad_in, low, ((1,), (1,))).astype(BF16)
        dk_ref[0, rows] = dot_f32(q_ref[rows], grad, ((1,), (1,))).astype(BF16)


def attention_backward(first, last, so_far, expo, datt, st, tops, q, k, v, scale):
    micro, heads, own, slots = expo.shape
    chunks, wide = datt.shape[1], datt.shape[3]
    steps = heads // PER
    at = lambda i: ((i + first) // steps, (i + first) % steps)
    flops = heads * 2 * 4 * own * slots * HD
    sts = st.shape[3]
    return pl.pallas_call(
        functools.partial(attention_backward_kernel, scale, first),
        grid=(last - first,),
        out_shape=(
            jax.ShapeDtypeStruct((micro, 1, heads, own, slots), BF16),
            jax.ShapeDtypeStruct((micro, chunks, heads * HD, wide), BF16),
            jax.ShapeDtypeStruct((micro, heads * HD, own), BF16),
            jax.ShapeDtypeStruct((micro, heads * HD, own), BF16),
            jax.ShapeDtypeStruct((micro, heads * HD, 128), F32),
        ),
        in_specs=[
            pl.BlockSpec((1, PER, own, slots), lambda i: (*at(i), 0, 0)),
            pl.BlockSpec((1, chunks, PER * HD, wide), lambda i: (at(i)[0], 0, at(i)[1], 0)),
            pl.BlockSpec((1, 1, chunks, sts, wide), lambda i: (at(i)[0], at(i)[1] * PER // GROUP, 0, 0, 0)),
            pl.BlockSpec((1, 1, chunks, 2 * GROUP, wide), lambda i: (at(i)[0], at(i)[1] * PER // GROUP, 0, 0, 0)),
            pl.BlockSpec((None, PER * HD, slots), lambda i: (*at(i), 0)),
            pl.BlockSpec((None, PER * HD, own), lambda i: (*at(i), 0)),
            pl.BlockSpec((None, PER * HD, own), lambda i: (*at(i), 0)),
        ]
        + [ANY] * len(so_far),
        out_specs=(
            pl.BlockSpec((1, 1, PER, own, slots), lambda i: (at(i)[0], 0, at(i)[1], 0, 0)),
            pl.BlockSpec((1, chunks, PER * HD, wide), lambda i: (at(i)[0], 0, at(i)[1], 0)),
            pl.BlockSpec((1, PER * HD, own), lambda i: (*at(i), 0)),
            pl.BlockSpec((1, PER * HD, own), lambda i: (*at(i), 0)),
            pl.BlockSpec((1, PER * HD, 128), lambda i: (*at(i), 0)),
        ),
        input_output_aliases={7 + i: i for i in range(len(so_far))},
        compiler_params=pltpu.CompilerParams(vmem_limit_bytes=VMEM_LIMIT),
        cost_estimate=pl.CostEstimate(
            flops=flops, bytes_accessed=heads * own * slots * 4, transcendentals=0
        ),
        name="attention_backward",
    )(expo, datt, st, tops, q, k, v, *so_far)


def shifted(arr, mesh_dims, dy, dx):
    if dy == 0 and dx == 0:
        return arr
    Y, X, _ = mesh_dims
    key = lambda y, x, c: (y * X + x) * 2 + c
    perm = [
        (key(y, x, c), key((y + dy) % Y, (x + dx) % X, c)) for y in range(Y) for x in range(X) for c in range(2)
    ]
    return lax.ppermute(arr, "keys", perm)


def late_weights_start(mesh_dims, own_first, own_last):
    Y, X, _ = mesh_dims
    first = [shifted(own_first, mesh_dims, 0, dx) for dx in range(X)]
    last = [shifted(own_last, mesh_dims, dy, 0) for dy in range(Y)]
    first_own = [shifted(own_first, mesh_dims, dy, 0) for dy in range(1, Y)]
    last_own = [shifted(own_last, mesh_dims, 0, dx) for dx in range(1, X)]
    return first, last, first_own, last_own


def late_weights_finish(mesh_dims, first, last, first_own, last_own):
    Y, X, _ = mesh_dims
    out = []
    for dy in range(Y):
        for dx in range(X):
            out.append(first_own[dy - 1] if dx == 0 and dy > 0 else shifted(first[dx], mesh_dims, dy, 0))
    for dy in range(Y):
        for dx in range(X):
            out.append(last_own[dx - 1] if dy == 0 and dx > 0 else shifted(last[dy], mesh_dims, 0, dx))
    return out


def late_grads_start(mesh_dims, send_a, keep_a, send_b, keep_b):
    Y, X, _ = mesh_dims
    first = [shifted(send_a[d - 1], mesh_dims, d, 0) for d in range(1, Y)]
    last = [shifted(send_b[d - 1], mesh_dims, 0, d) for d in range(1, X)]
    return (keep_a, first), (keep_b, last)


def late_grads_finish(mesh_dims, first, last):
    Y, X, _ = mesh_dims
    key = lax.axis_index("keys")
    x, y = (key // 2) % X, key // (2 * X)

    def line(keep, got, place, move):
        total = keep.astype(F32)
        for piece in got:
            total = total + piece.astype(F32)
        total = total.astype(BF16)
        count = total.shape[0]
        pick = lambda d: lax.dynamic_index_in_dim(total, (place + d) % count, 0, keepdims=False)
        return [total] + [move(pick(d), d) for d in range(1, count)]

    return (
        line(*first, x, lambda a, d: shifted(a, mesh_dims, 0, d)),
        line(*last, y, lambda a, d: shifted(a, mesh_dims, d, 0)),
    )


def halves(value):
    high = value.astype(BF16)
    return high, (value - high.astype(F32)).astype(BF16)


def update_weights_kernel(
    block_ids, first_column, fixes, late_ref, early_ref, basis_ref, master_ref, one_ref, two_ref,
    grad_out, one_out, two_out, master_out, copy_out, joined,
):
    s = pl.program_id(0)
    block = block_ids[s]
    early = early_ref[jnp.minimum(block, EARLY - 1)].astype(F32)
    share = early.shape[1]
    for i in range(early.shape[0]):
        joined[i * share : (i + 1) * share] = early[i]
    grad = jnp.where(block < EARLY, joined[...], late_ref[0])
    grad_out[0] = grad
    basis = basis_ref[0]
    basis_high, basis_low = halves(basis)

    def product(value, contract):
        n = value.shape[0]
        high, rest = halves(value)
        both = dot_f32(jnp.concatenate([high, rest], axis=0), basis_high, contract)
        return both[:n] + (both[n:] + dot_f32(high, basis_low, contract))

    rotated = product(grad, ((1,), (0,)))
    new_one = BETA_ONE * one_ref[0] + (1.0 - BETA_ONE) * rotated
    new_two = BETA_TWO * two_ref[0] + (1.0 - BETA_TWO) * rotated * rotated
    one_out[0] = new_one
    two_out[0] = new_two
    direction = new_one / fixes[0] / (jnp.sqrt(new_two / fixes[1]) + EPS_ADAM)
    back = product(direction, ((1,), (1,)))
    columns = first_column[s] + lax.broadcasted_iota(jnp.int32, (grad.shape[0], 1), 0)
    master = master_ref[0]
    new_master = master - column_rates(columns) * (back + DECAY * master)
    master_out[0] = new_master
    copy_out[0] = new_master.astype(BF16)


def update_weights(block_ids, first_column, fixes, late, early, basis, master, one, two):
    slots_here, n, width = master.shape
    mat = pl.BlockSpec((1, n, width), lambda s: (s, 0, 0))
    smem = pl.BlockSpec(memory_space=pltpu.SMEM)
    return pl.pallas_call(
        update_weights_kernel,
        grid=(slots_here,),
        out_shape=tuple(jax.ShapeDtypeStruct(master.shape, F32) for _ in range(4))
        + (jax.ShapeDtypeStruct(master.shape, BF16),),
        in_specs=[smem, smem, smem, mat, pl.BlockSpec(early.shape, lambda s: (0, 0, 0, 0)),
                  pl.BlockSpec((1, width, width), lambda s: (s, 0, 0)), mat, mat, mat],
        out_specs=(mat,) * 5,
        scratch_shapes=[pltpu.VMEM((n, width), F32)],
        compiler_params=pltpu.CompilerParams(vmem_limit_bytes=VMEM_LIMIT),
        name="update_weights",
    )(block_ids, first_column, fixes, late, early, basis, master, one, two)


def to_chunks(arr, chunks):
    pieces, rows, own = arr.shape[-3:]
    lead = arr.shape[:-3]
    if pieces == chunks:
        return arr
    per = pieces // chunks
    arr = arr.reshape(lead + (chunks, per, rows, own))
    return jnp.moveaxis(arr, -3, -2).reshape(lead + (chunks, rows, per * own))


def from_chunks(arr, pieces):
    chunks, rows, wide = arr.shape[-3:]
    lead = arr.shape[:-3]
    if pieces == chunks:
        return arr
    per = pieces // chunks
    arr = arr.reshape(lead + (chunks, rows, per, wide // per))
    return jnp.moveaxis(arr, -2, -3).reshape(lead + (pieces, rows, wide // per))


def per_device(
    mesh_dims,
    tokens,
    prev_logits,
    segments,
    out_cot,
    master_mat,
    mom1_mat,
    mom2_mat,
    eigen_bases,
    master_small,
    mom1_small,
    mom2_small,
    owners,
    step_count,
):
    Y, X, R = mesh_dims
    keys = Y * X * 2
    micro, row_count, key_len, width = tokens.shape
    slot_count = prev_logits.shape[4]
    slots_here, _, cols_here = master_mat.shape
    blocks = slots_here * R
    token_count = micro * key_len
    scale = HD ** (-0.5)
    key_index = lax.axis_index("keys")
    row_index = lax.axis_index("rows")
    wide = max(key_len, min(256, slot_count))
    chunks = slot_count // wide
    groups = H // GROUP

    x_own = tokens.reshape(micro, key_len, width)
    w_own = jnp.swapaxes(master_mat, 1, 2)
    small_low = master_small.astype(BF16).reshape(1, slots_here * cols_here)
    ext = lax.dynamic_update_slice(
        jnp.zeros((EXT, width), BF16), small_low, (row_index, jnp.int32(0))
    )
    fast = cols_here % 16 == 0
    wt, *w_late, ext_all, xg = gather_weights(mesh_dims, owners, w_own, ext, x_own)
    if fast:
        pieces = late_weights_start(mesh_dims, *w_late)
    else:
        late = [lax.all_gather(jnp.concatenate(w_late), "keys", axis=1).reshape(2 * FF + width, width)]
    w_t = wt.reshape(EARLY * BLOCK_COLUMNS, width)
    small_all = ext_all.reshape(keys, EXT, width)[:, :R, : slots_here * cols_here]
    params = (
        jnp.transpose(small_all.reshape(keys, R, slots_here, cols_here), (1, 2, 0, 3))
        .reshape(blocks * GAIN_ROW_WIDTH)
        .astype(F32)
    )
    bias_q = params[:width]
    bias_v = params[width : 2 * width]
    bias_o = params[2 * width : 3 * width]
    gain_one = params[3 * width : 4 * width]
    shift_one = params[4 * width : 5 * width]
    bias_up = params[5 * width : 5 * width + FF]
    bias_down = params[5 * width + FF : 6 * width + FF]
    gain_two = params[6 * width + FF : 7 * width + FF]
    shift_two = params[7 * width + FF :]

    vec = jnp.stack([bias_o, gain_one, shift_one, bias_down, gain_two, shift_two, bias_q, bias_v])
    q_all, k_all, v_all = project(xg.reshape(micro, slot_count, width), x_own, w_t, vec, scale)
    x_rows = x_own.reshape(token_count, width)

    seg_rows = segments.reshape(micro, slot_count)
    seg_keys = lax.dynamic_slice_in_dim(seg_rows, key_index * key_len, key_len, 1)
    forward = ()
    for m in range(micro):
        forward = attention_forward(
            m, forward, q_all, k_all, v_all, prev_logits,
            seg_keys[:, :, None], seg_rows[:, None, :], chunks, wide,
        )
        if m == 0 and fast:
            forward, first, last = lax.optimization_barrier((tuple(forward), *pieces[:2]))
            late = late_weights_finish(mesh_dims, first, last, *pieces[2:])
    logits, expo, o_part, st_part, tops = forward
    o_part = from_chunks(o_part, keys).reshape(micro, Y, X, 2, width, key_len)
    st_part = from_chunks(st_part, keys).reshape(micro, groups, Y, X, 2, 2 * GROUP, key_len)
    out_hidden, datt_all, st_all, grad_one, dvec, d_bias_up, *dw_late = middle(
        mesh_dims, o_part, st_part, x_own, out_cot.reshape(x_own.shape), late, vec, bias_up[None]
    )
    out_hidden = out_hidden.reshape(tokens.shape)
    datt_all = to_chunks(datt_all.reshape(micro, keys, width, key_len), chunks)
    st_all = to_chunks(st_all.reshape(micro, groups, keys, STAT_ROWS, key_len), chunks)
    so_far = ()
    if fast:
        first, last = late_grads_start(mesh_dims, *dw_late)
    steps = micro * (H // PER)
    turns = (0, steps * 5 // 8, steps)
    for turn in range(2):
        so_far = attention_backward(
            turns[turn], turns[turn + 1], so_far, expo, datt_all, st_all, tops, q_all, k_all, v_all, scale
        )
        if turn == 0 and fast:
            so_far, first, last = lax.optimization_barrier((tuple(so_far), first, last))
            fin = late_grads_finish(mesh_dims, first, last)
    grad_prev, dq_part, dk, dv, dq_sum = so_far
    dq_part = from_chunks(dq_part, keys).reshape(micro, Y, X, 2, width, key_len)
    inverse = inverse_order(owners)
    slot_index_list = row_index * slots_here + jnp.arange(slots_here, dtype=jnp.int32)
    block_ids = jnp.take(inverse, slot_index_list)
    if fast:
        grad_tokens, mine_late, mine_early, small_sum = tail(
            mesh_dims, inverse, dq_part, dk, dv, x_own, grad_one, wt, *fin, dvec, d_bias_up,
            xg.reshape(micro, slot_count, width), dq_sum,
        )
    else:
        dq = lax.psum_scatter(
            dq_part.reshape(micro, keys, width, key_len), "keys", scatter_dimension=1, tiled=True
        ).reshape(micro, width, key_len)
        grad_proj = jnp.swapaxes(jnp.concatenate([dq, dk, dv], axis=1), 0, 1).reshape(
            3 * width, token_count
        )
        d_qkv = dot_f32(grad_proj, x_rows, ((1,), (0,))).astype(BF16)
        grad_tokens = (
            grad_one.reshape(token_count, width) + dot_f32(grad_proj, w_t, ((0,), (0,)))
        ).astype(BF16)
        sums = jnp.sum(grad_proj.astype(F32).reshape(3, width, token_count), axis=2)
        small_sum = lax.psum(
            jnp.concatenate(
                [sums[0][None], sums[2][None], dvec[:3], d_bias_up.reshape(FF // width, width), dvec[3:6]]
            ),
            ("rows", "keys"),
        )
        grads = jnp.concatenate([d_qkv, dw_late[0]], axis=0).reshape(blocks, keys, cols_here, width)
        grads = lax.psum_scatter(grads, "keys", scatter_dimension=1, tiled=True)
        grads = jnp.take(grads.reshape(blocks, cols_here, width), inverse, axis=0)
        mine_t = lax.psum_scatter(grads, "rows", scatter_dimension=0, tiled=True).astype(F32)
    grad_tokens = grad_tokens.reshape(tokens.shape)
    flat = small_sum.reshape(-1)[: blocks * GAIN_ROW_WIDTH].reshape(blocks, GAIN_ROW_WIDTH)
    mine_small = lax.dynamic_slice(
        flat, (row_index * slots_here, key_index * cols_here), (slots_here, cols_here)
    )

    steps_done = step_count[0].astype(F32)
    fix_one = 1.0 - jnp.power(jnp.asarray(BETA_ONE, F32), steps_done)
    fix_two = 1.0 - jnp.power(jnp.asarray(BETA_TWO, F32), steps_done)
    if fast:
        first_column = block_ids * BLOCK_COLUMNS + key_index * cols_here
        mats = [jnp.swapaxes(a, 1, 2) for a in (master_mat, mom1_mat, mom2_mat)]
        updated = update_weights(
            block_ids, first_column, jnp.stack([fix_one, fix_two]), mine_late, mine_early, eigen_bases, *mats
        )
        mine_mat, new_one, new_two, new_master, copy_mat = (jnp.swapaxes(a, 1, 2) for a in updated)
    else:
        mine_mat = jnp.swapaxes(mine_t, 1, 2)
        rotated = jnp.einsum("sed,sec->sdc", eigen_bases, mine_mat, precision=HIGHEST_PREC)
        new_one = BETA_ONE * mom1_mat + (1.0 - BETA_ONE) * rotated
        new_two = BETA_TWO * mom2_mat + (1.0 - BETA_TWO) * rotated * rotated
        direction = new_one / fix_one / (jnp.sqrt(new_two / fix_two) + EPS_ADAM)
        back_rot = jnp.einsum("sdk,skc->sdc", eigen_bases, direction, precision=HIGHEST_PREC)
        columns = (
            block_ids[:, None] * (cols_here * keys)
            + key_index * cols_here
            + jnp.arange(cols_here, dtype=jnp.int32)[None, :]
        )
        rates = column_rates(columns)[:, None, :]
        new_master = master_mat - rates * (back_rot + DECAY * master_mat)
        copy_mat = new_master.astype(BF16)
    small_one = BETA_ONE * mom1_small + (1.0 - BETA_ONE) * mine_small
    small_two = BETA_TWO * mom2_small + (1.0 - BETA_TWO) * mine_small * mine_small
    new_small = master_small - RATE_SMALL * (small_one / fix_one) / (
        jnp.sqrt(small_two / fix_two) + EPS_ADAM
    )
    return (
        out_hidden,
        logits,
        grad_tokens,
        grad_prev,
        mine_mat,
        new_one,
        new_two,
        new_master,
        copy_mat,
        mine_small,
        small_one,
        small_two,
        new_small,
        new_small.astype(BF16),
    )


def solution(mesh):
    chips = mesh.shape["keys"] // 2
    side = math.isqrt(chips)
    dims = (side, side, mesh.shape["rows"]) if side * side == chips else (1, chips, mesh.shape["rows"])
    acts = P(None, "rows", "keys", None)
    scores = P(None, "rows", None, "keys", None)
    mats = P("rows", None, "keys")
    smalls = P("rows", "keys")
    return jax.shard_map(
        functools.partial(per_device, dims),
        mesh=mesh,
        in_specs=(
            acts, scores, P(None, "rows", None), acts, mats, mats, mats,
            P("rows", None, None), smalls, smalls, smalls, P(), P(),
        ),
        out_specs=(acts, scores, acts, scores) + (mats,) * 5 + (smalls,) * 5,
        check_vma=False,
    )
```

profile of v0, /device:TPU:8, one launch (start us, length us, event | category | flops | bytes accessed | tf_op | source)
XLA Modules:
  0.0 332.3 jit_solution(16867072707042163904)
XLA Ops:
  0.6 0.7 convert_element_type.41
  2.3 52.2 %gather_weights.1 = (bf16[2,2,2,2,144,768]{5,4,3,2,1,0:T(8,128)(2,1)}, bf16[3,144,768]{2,1,0:T(8,128)(2,1)}, bf16[3,144,768]{2,1,0:T(8,128)(2,1)}, bf16[2,2,2,16...) custom-call(s32[8]{0:T(128)} %owners.1, f32[2,144,768]{2,1,0:T(8,128)} %bitcast.50, bf16[16,768]{1,0:T(8,128)(2,1)} %copy-done.16, ...), custom_call_target="tpu_custom_call" | custom-call | tf_op jit(solution)/shard_map/gather_weights/pallas_call | solution.py:311
  54.5 1.6 collective-permute-start
  56.6 1.5 collective-permute-start.1
  58.6 0.8 slice.47
  59.8 0.7 dynamic-slice_reduce_fusion
  60.5 0.8 broadcast_in_dim.18.segk_ref
  61.3 0.6 stack.40.vec_ref.refs_4_
  61.9 12.1 %project.1 = (bf16[2,768,2048]{2,1,0:T(8,128)(2,1)}, bf16[2,768,256]{2,1,0:T(8,128)(2,1)}, bf16[2,768,256]{2,1,0:T(8,128)(2,1)}) custom-call(bf16[2,2048,768]{2,1,0:T(8,128)(2,1)} %bitcast.48, bf16[2,256,768]{2,1,0:T(8,128)(2,1)} %bitcast.45, bf16[2304,768]{1,0:T(8,128)(2,1)} %bitcast.52, f32[8,768]{1,0:T(8,128)} %stack.40.vec_ref.refs_4_), custom_call_target="tpu_custom_call" | custom-call | flops 6039797760 | bytes 12582912 | tf_op jit(solution)/shard_map/project/pallas_call | solution.py:1300
  74.1 20.6 %attention_forward.2 = (bf16[2,1,12,256,2048]{4,3,2,1,0:T(8,128)(2,1)}, bf16[2,12,256,2048]{3,2,1,0:T(8,128)(2,1)}, bf16[2,8,768,256]{3,2,1,0:T(8,128)(2,1)}, f3...) custom-call(bf16[2,768,2048]{2,1,0:T(8,128)(2,1)} %get-tuple-element.82.q_ref, ...), custom_call_target="tpu_custom_call" | custom-call | flops 1610612736 | bytes 37748736 | tf_op jit(solution)/shard_map/attention_forward/pallas_call | solution.py:1365
  94.7 1.6 collective-permute-start.3
  97.4 20.6 %attention_forward.3 = (bf16[2,1,12,256,2048]{4,3,2,1,0:T(8,128)(2,1)}, bf16[2,12,256,2048]{3,2,1,0:T(8,128)(2,1)}, bf16[2,8,768,256]{3,2,1,0:T(8,128)(2,1)}, f3...) custom-call(bf16[2,768,2048]{2,1,0:T(8,128)(2,1)} %get-tuple-element, ...), custom_call_target="tpu_custom_call", output_to_operand_aliasing={{0}: (6, {}), {1}: (7, {}), {2}: (8, {}), {3}: (9, {}), {4}... | custom-call | flops 1610612736 | bytes 37748736 | tf_op jit(solution)/shard_map/attention_forward/pallas_call | solution.py:1365
  118.1 0.8 copy-done.10
  119.4 74.7 %middle.1 = (bf16[2,256,768]{2,1,0:T(8,128)(2,1)}, bf16[2,2,2,2,768,256]{5,4,3,2,1,0:T(8,128)(2,1)}, f32[2,4,2,2,2,8,256]{6,5,4,3,2,1,0:T(8,128)}, f32[2,256,768...) custom-call(bf16[2,2,2,2,768,256]{5,4,3,2,1,0:T(8,128)(2,1)} %bitcas, ...), custom_call_target="tpu_custom_call" | custom-call | tf_op jit(solution)/shard_map/middle/pallas_call | solution.py:843
  194.1 2.3 collective-permute-start.6
  196.6 22.2 %attention_backward.2 = (bf16[2,1,12,256,2048]{4,3,2,1,0:T(8,128)(2,1)}, bf16[2,8,768,256]{3,2,1,0:T(8,128)(2,1)}, bf16[2,768,256]{2,1,0:T(8,128)(2,1)}, bf16[2,768,256]{2,1,0:T(8,128)(2,1)}, f32[2,768,128]{2,1,0:T(8,128)}) custom-call(bf16[2,12,256,2048]{3,2,1,0:T(8,128)(2,1)} %get-tuple-element.105.e_ref, bf16[2,8,768,256]{3,2,1,0:T(8,128)(2,1)} %bitcast.40, ...), custom_call_target="tpu_custom_call" | custom-call | flops 3221225472 | bytes 25165824 | tf_op jit(solution)/shard_map/attention_backward/pallas_call | solution.py:1440
  218.8 7.6 %collective-permute-done.6 = bf16[2,3,144,768]{3,2,1,0:T(8,128)(2,1)S(1)} collective-permute-done((bf16[2,3,144,768]{3,2,1,0:T(8,128)(2,1)}, bf16[2,3,144,768]{3,2,1,0:T(8,128)(2,1)S(1)}, u32[]{:S(2)}, u32[]{:S(2)}) %collective-permute-start.6) | collective-permute-done | bytes 1327136 | tf_op jit(solution)/shard_map/ppermute | solution.py:1484
  226.6 0.9 copy-done.5
  227.5 1.8 add_convert_fusion.refs_2_
  229.3 1.0 dynamic-slice_bitcast_fusion
  230.3 0.7 collective-permute-start.9
  231.4 1.0 dynamic-slice_bitcast_fusion.1
  232.4 1.3 collective-permute-start.8
  234.3 0.6 gather_fusion
  236.2 14.9 %attention_backward.3 = (bf16[2,1,12,256,2048]{4,3,2,1,0:T(8,128)(2,1)}, bf16[2,8,768,256]{3,2,1,0:T(8,128)(2,1)}, bf16[2,768,256]{2,1,0:T(8,128)(2,1)}, bf16[2,768,256]{2,1,0:T(8,128)(2,1)}, f32[2,768,128]{2,1,0:T(8,128)}) custom-call(bf16[2,12,256,2048]{3,2,1,0:T(8,128)(2,1)} %get-tuple-el, ...), custom_call_target="tpu_custom_call", output_to_operand_aliasing={{0}: (7, {}), {1}: (8, {}), {2}: (9, {}), {3}: (10, {}), {4... | custom-call | flops 3221225472 | bytes 25165824 | tf_op jit(solution)/shard_map/attention_backward/pallas_call | solution.py:1440
  251.1 0.8 copy-done.13
  252.2 69.0 %tail.1 = (bf16[2,256,768]{2,1,0:T(8,128)(2,1)}, f32[2,144,768]{2,1,0:T(8,128)}, bf16[2,4,36,768]{3,2,1,0:T(8,128)(2,1)}, f32[16,768]{1,0:T(8,128)}) custom-call(s32[8]{0:T(128)} %copy-done, bf16[2,2,2,2,768,256]{5,4,3,2,1,0:T(8,128)(2,1)} %bitcast.43, bf16[2,768,256]{2,1,0:T(8,128)(2,1)} %get-tuple-element.124.dk_hbm, ...), custom_call_target="tpu_custom_call" | custom-call | tf_op jit(solution)/shard_map/tail/pallas_call | solution.py:1217
  321.2 0.8 reshape.125
  322.0 0.7 fusion.2
  322.7 7.8 %update_weights.1 = (f32[2,144,768]{2,1,0:T(8,128)}, f32[2,144,768]{2,1,0:T(8,128)}, f32[2,144,768]{2,1,0:T(8,128)}, f32[2,144,768]{2,1,0:T(8,128)}, bf16[2,144,768]{2,1,0:T(8,128)(2,1)}) custom-call(s32[2]{0:T(128)} %get-tuple-element.206.block_ids, s32[2]{0:T(128)} %get-tuple-element.205.first_column, f32[2]{0:T(128)} %pad_maximum_fusion.fixes, ...), custom_call_target="tpu_custom_call" | custom-call | tf_op jit(solution)/shard_map/update_weights/pallas_call | solution.py:1579
  330.5 0.9 copy.71
  331.4 0.9 copy.72
  (75 shorter events, 6.0 us)
Async XLA Ops:
  1.7 0.6 copy-start.16
  54.5 40.2 %collective-permute-start = (bf16[3,144,768]{2,1,0:T(8,128)(2,1)}, bf16[3,144,768]{2,1,0:T(8,128)(2,1)S(1)}, u32[]{:S(2)}, u32[]{:S(2)}) collective-permute-start(bf16[3,144,768]{2,1,0:T(8,128)(2,1)} %get-tuple-element.99.refs_6_), channel_id=1, source_target_pairs={{0,2},{1,3},{2,0},{3,1},{4,6},{5,7},{6,4},{7,5},{8,10},{9,11},{10,... | collective-permute-start | bytes 1990664 | tf_op jit(solution)/shard_map/ppermute | solution.py:1484
  56.0 62.0 %collective-permute-start.2 = (bf16[3,144,768]{2,1,0:T(8,128)(2,1)}, bf16[3,144,768]{2,1,0:T(8,128)(2,1)S(1)}, u32[]{:S(2)}, u32[]{:S(2)}) collective-permute-start(bf16[3,144,768]{2,1,0:T(8,128)(2,1)} %get-tuple-element.99.refs_6_), channel_id=1, source_target_pairs={{0,4},{1,5},{2,6},{3,7},{4,0},{5,1},{6,2},{7,3},{8,12},{9,13},{10,... | collective-permute-start | bytes 1990664 | tf_op jit(solution)/shard_map/ppermute | solution.py:1484
  56.6 38.2 %collective-permute-start.1 = (bf16[3,144,768]{2,1,0:T(8,128)(2,1)}, bf16[3,144,768]{2,1,0:T(8,128)(2,1)S(1)}, u32[]{:S(2)}, u32[]{:S(2)}) collective-permute-start(bf16[3,144,768]{2,1,0:T(8,128)(2,1)} %get-tuple-element.101.refs_10_), channel_id=1, source_target_pairs={{0,4},{1,5},{2,6},{3,7},{4,0},{5,1},{6,2},{7,3},{8,12},{9,13},{10,... | collective-permute-start | bytes 1990664 | tf_op jit(solution)/shard_map/ppermute | solution.py:1484
  58.1 60.0 %collective-permute-start.4 = (bf16[3,144,768]{2,1,0:T(8,128)(2,1)}, bf16[3,144,768]{2,1,0:T(8,128)(2,1)S(1)}, u32[]{:S(2)}, u32[]{:S(2)}) collective-permute-start(bf16[3,144,768]{2,1,0:T(8,128)(2,1)} %get-tuple-element.101.refs_10_), channel_id=1, source_target_pairs={{0,2},{1,3},{2,0},{3,1},{4,6},{5,7},{6,4},{7,5},{8,10},{9,11},{10,... | collective-permute-start | bytes 1990664 | tf_op jit(solution)/shard_map/ppermute | solution.py:1484
  94.7 23.4 %copy-start.9 = (bf16[3,144,768]{2,1,0:T(8,128)(2,1)}, bf16[3,144,768]{2,1,0:T(8,128)(2,1)S(1)}, u32[]{:S(2)}) copy-start(bf16[3,144,768]{2,1,0:T(8,128)(2,1)S(1)} %collective-permute-done.refs_7_) | copy-start | bytes 1990660
  94.7 23.3 %copy-start.11 = (bf16[3,144,768]{2,1,0:T(8,128)(2,1)}, bf16[3,144,768]{2,1,0:T(8,128)(2,1)S(1)}, u32[]{:S(2)}) copy-start(bf16[3,144,768]{2,1,0:T(8,128)(2,1)S(1)} %collective-permute-done.1.refs_12_) | copy-start | bytes 1990660
  94.7 23.4 %collective-permute-start.3 = (bf16[3,144,768]{2,1,0:T(8,128)(2,1)S(1)}, bf16[3,144,768]{2,1,0:T(8,128)(2,1)S(1)}, u32[]{:S(2)}, u32[]{:S(2)}) collective-permute-start(bf16[3,144,768]{2,1,0:T(8,128)(2,1)S(1)} %collective-permute-done.refs_7_), channel_id=1, source_target_pairs={{0,4},{1,5},{2,6},{3,7},{4,0},{5,1},{6,2},{7,3},{8,12},{9,13},{10,... | collective-permute-start | bytes 1990664 | tf_op jit(solution)/shard_map/ppermute | solution.py:1484
  96.3 21.9 %collective-permute-start.5 = (bf16[3,144,768]{2,1,0:T(8,128)(2,1)S(1)}, bf16[3,144,768]{2,1,0:T(8,128)(2,1)}, u32[]{:S(2)}, u32[]{:S(2)}) collective-permute-start(bf16[3,144,768]{2,1,0:T(8,128)(2,1)S(1)} %collective-permute-done.1.refs_12_), channel_id=1, source_target_pairs={{0,2},{1,3},{2,0},{3,1},{4,6},{5,7},{6,4},{7,5},{8,10},{9,11},{10,... | collective-permute-start | bytes 1990664 | tf_op jit(solution)/shard_map/ppermute | solution.py:1484
  118.1 0.8 copy-start.10
  118.1 1.0 copy-start.12
  118.1 1.2 copy-start.15
  119.4 77.1 %copy-start.20 = (s32[8]{0:T(128)S(1)}, s32[8]{0:T(128)}, u32[]{:S(2)}) copy-start(s32[8]{0:T(128)} %owners.1) | copy-start | bytes 100
  194.1 32.3 %collective-permute-start.6 = (bf16[2,3,144,768]{3,2,1,0:T(8,128)(2,1)}, bf16[2,3,144,768]{3,2,1,0:T(8,128)(2,1)S(1)}, u32[]{:S(2)}, u32[]{:S(2)}) collective-permute-start(bf16[2,3,144,768]{3,2,1,0:T(8,128)(2,1)} %bitcast.67), channel_id=1, source_target_pairs={{0,4},{1,5},{2,6},{3,7},{4,0},{5,1},{6,2},{7,3},{8,12},{9,13},{10,... | collective-permute-start | bytes 3981320 | tf_op jit(solution)/shard_map/ppermute | solution.py:1484
  196.3 30.2 %collective-permute-start.7 = (bf16[2,3,144,768]{3,2,1,0:T(8,128)(2,1)}, bf16[2,3,144,768]{3,2,1,0:T(8,128)(2,1)}, u32[]{:S(2)}, u32[]{:S(2)}) collective-permute-start(bf16[2,3,144,768]{3,2,1,0:T(8,128)(2,1)} %bitcast.66), channel_id=1, source_target_pairs={{0,2},{1,3},{2,0},{3,1},{4,6},{5,7},{6,4},{7,5},{8,10},{9,11},{10,... | collective-permute-start | bytes 3981320 | tf_op jit(solution)/shard_map/ppermute | solution.py:1484
  196.6 37.7 %copy-start = (s32[8]{0:T(128)}, s32[8]{0:T(128)S(1)}, u32[]{:S(2)}) copy-start(s32[8]{0:T(128)S(1)} %select_reduce_fusion.inverse) | copy-start | bytes 100
  196.6 30.9 %copy-start.4 = (bf16[2,3,144,768]{3,2,1,0:T(8,128)(2,1)S(1)}, bf16[2,3,144,768]{3,2,1,0:T(8,128)(2,1)}, u32[]{:S(2)}) copy-start(bf16[2,3,144,768]{3,2,1,0:T(8,128)(2,1)} %get-tuple-element.132) | copy-start | bytes 3981316
  226.4 1.1 copy-start.5
  227.5 3.6 %copy-start.3 = (bf16[2,3,144,768]{3,2,1,0:T(8,128)(2,1)S(1)}, bf16[2,3,144,768]{3,2,1,0:T(8,128)(2,1)}, u32[]{:S(2)}) copy-start(bf16[2,3,144,768]{3,2,1,0:T(8,128)(2,1)} %get-tuple-element.130) | copy-start | bytes 3981316
  227.5 3.6 %copy-start.6 = (bf16[2,3,144,768]{3,2,1,0:T(8,128)(2,1)S(1)}, bf16[2,3,144,768]{3,2,1,0:T(8,128)(2,1)}, u32[]{:S(2)}) copy-start(bf16[2,3,144,768]{3,2,1,0:T(8,128)(2,1)} %copy-done.5) | copy-start | bytes 3981316
  229.3 2.1 copy-start.1
  230.3 20.8 %collective-permute-start.9 = (bf16[3,144,768]{2,1,0:T(8,128)(2,1)}, bf16[3,144,768]{2,1,0:T(8,128)(2,1)S(1)}, u32[]{:S(2)}, u32[]{:S(2)}) collective-permute-start(bf16[3,144,768]{2,1,0:T(8,128)(2,1)} %dynamic-slice_bitcast_fusion), channel_id=1, source_target_pairs={{0,4},{1,5},{2,6},{3,7},{4,0},{5,1},{6,2},{7,3},{8,12},{9,13},{10,... | collective-permute-start | bytes 1990664 | tf_op jit(solution)/shard_map/ppermute | solution.py:1484
  231.4 19.7 %copy-start.2 = (bf16[2,3,144,768]{3,2,1,0:T(8,128)(2,1)}, bf16[2,3,144,768]{3,2,1,0:T(8,128)(2,1)S(1)}, u32[]{:S(2)}) copy-start(bf16[2,3,144,768]{3,2,1,0:T(8,128)(2,1)S(1)} %add_convert_fusion.1.refs_0_) | copy-start | bytes 3981316
  232.4 18.7 %collective-permute-start.8 = (bf16[3,144,768]{2,1,0:T(8,128)(2,1)}, bf16[3,144,768]{2,1,0:T(8,128)(2,1)S(1)}, u32[]{:S(2)}, u32[]{:S(2)}) collective-permute-start(bf16[3,144,768]{2,1,0:T(8,128)(2,1)} %dynamic-slice_bitcast_fusion.1), channel_id=1, source_target_pairs={{0,2},{1,3},{2,0},{3,1},{4,6},{5,7},{6,4},{7,5},{8,10},{9,11},{10,... | collective-permute-start | bytes 1990664 | tf_op jit(solution)/shard_map/ppermute | solution.py:1484
  251.1 0.8 copy-start.13
  251.1 1.0 copy-start.14
  252.2 69.8 %copy-start.17 = (f32[2,144]{1,0:T(2,128)S(1)}, f32[2,144]{1,0:T(2,128)}, u32[]{:S(2)}) copy-start(f32[2,144]{1,0:T(2,128)} %param.21) | copy-start | bytes 3460
  252.2 69.9 %copy-start.18 = (f32[2,144]{1,0:T(2,128)S(1)}, f32[2,144]{1,0:T(2,128)}, u32[]{:S(2)}) copy-start(f32[2,144]{1,0:T(2,128)} %param.23) | copy-start | bytes 3460
  252.2 69.9 %copy-start.19 = (f32[2,144]{1,0:T(2,128)S(1)}, f32[2,144]{1,0:T(2,128)}, u32[]{:S(2)}) copy-start(f32[2,144]{1,0:T(2,128)} %param.22) | copy-start | bytes 3460
  322.7 7.8 %copy-start.7 = (bf16[2,256,768]{2,1,0:T(8,128)(2,1)S(1)}, bf16[2,256,768]{2,1,0:T(8,128)(2,1)}, u32[]{:S(2)}) copy-start(bf16[2,256,768]{2,1,0:T(8,128)(2,1)} %get-tuple-element.103) | copy-start | bytes 2359300
  322.7 8.7 %copy-start.8 = (bf16[2,256,768]{2,1,0:T(8,128)(2,1)S(1)}, bf16[2,256,768]{2,1,0:T(8,128)(2,1)}, u32[]{:S(2)}) copy-start(bf16[2,256,768]{2,1,0:T(8,128)(2,1)} %get-tuple-element.134) | copy-start | bytes 2359300
where the time goes:
time: 334 us; the launch traced here: 332 us
  Pallas kernels  294 us (88%)
  local copies, waits for them, and re-layouts  13.2 us (4%)
  starting transfers between devices  10.6 us (3%)
  waiting for transfers between devices  7.79 us (2%)
  other arithmetic  4.78 us (1%)
    pallas_call x1, Pallas kernels, middle(): pl.pallas_call(functools.partial(middle_kernel, Y, X, R, blocks, pieces),...  74.7 us
    pallas_call x1, Pallas kernels, tail(): pl.pallas_call(functools.partial(tail_kernel, Y, X, R), out_shape=(jax.Sh...  69 us
    pallas_call x1, Pallas kernels, gather_weights(): pl.pallas_call(functools.partial(gather_weights_kernel, Y, X, R), out_sha...  52.2 us
    pallas_call x2, Pallas kernels, attention_forward(): pl.pallas_call(attention_forward_kernel, grid=(heads // PER,), out_shape=...  41.2 us
    pallas_call x2, Pallas kernels, attention_backward(): pl.pallas_call(functools.partial(attention_backward_kernel, scale, first)...  37.1 us
    pallas_call x1, Pallas kernels, project(): pl.pallas_call(functools.partial(project_kernel, scale), grid=(micro, slo...  12.1 us
    ppermute x10, starting transfers between devices, shifted(): return lax.ppermute(arr, 'keys', perm)  10.6 us
    pallas_call x1, Pallas kernels, update_weights(): pl.pallas_call(update_weights_kernel, grid=(slots_here,), out_shape=tuple...  7.8 us
  transfers between devices with their start and end apart: 10, of which 2 were waited for; matrix products, arithmetic and copies ran while one was open for 2% of the time, Pallas kernels for 27%

commit v1 on v0

--- a/solution.py
+++ b/solution.py
@@ -1697,7 +1697,7 @@
     if fast:
         first, last = late_grads_start(mesh_dims, *dw_late)
     steps = micro * (H // PER)
-    turns = (0, steps * 5 // 8, steps)
+    turns = (0, steps * 6 // 8, steps)
     for turn in range(2):
         so_far = attention_backward(
             turns[turn], turns[turn + 1], so_far, expo, datt_all, st_all, tops, q_all, k_all, v_all, scale

time: 334 us -> 332 us (level)
  transfers between devices with their start and end apart: 10 -> 10, of which waited for: 2 -> 3; matrix products, arithmetic and copies ran while one was open for 2% -> 2% of each run, Pallas kernels for 27% -> 27%
where the time goes in v1:
time: 332 us; the launch traced here: 330 us
  Pallas kernels  294 us (89%)
  local copies, waits for them, and re-layouts  13 us (4%)
  starting transfers between devices  10.6 us (3%)
  waiting for transfers between devices  5.51 us (2%)
  other arithmetic  4.78 us (1%)
    pallas_call x1, Pallas kernels, middle(): pl.pallas_call(functools.partial(middle_kernel, Y, X, R, blocks, pieces),...  74.7 us
    pallas_call x1, Pallas kernels, tail(): pl.pallas_call(functools.partial(tail_kernel, Y, X, R), out_shape=(jax.Sh...  69.2 us
    pallas_call x1, Pallas kernels, gather_weights(): pl.pallas_call(functools.partial(gather_weights_kernel, Y, X, R), out_sha...  52.2 us
    pallas_call x2, Pallas kernels, attention_forward(): pl.pallas_call(attention_forward_kernel, grid=(heads // PER,), out_shape=...  41.2 us
    pallas_call x2, Pallas kernels, attention_backward(): pl.pallas_call(functools.partial(attention_backward_kernel, scale, first)...  37.1 us
    pallas_call x1, Pallas kernels, project(): pl.pallas_call(functools.partial(project_kernel, scale), grid=(micro, slo...  12.1 us
    ppermute x10, starting transfers between devices, shifted(): return lax.ppermute(arr, 'keys', perm)  10.6 us
    pallas_call x1, Pallas kernels, update_weights(): pl.pallas_call(update_weights_kernel, grid=(slots_here,), out_shape=tuple...  7.8 us
  transfers between devices with their start and end apart: 10, of which 3 were waited for; matrix products, arithmetic and copies ran while one was open for 2% of the time, Pallas kernels for 27%

profile of v1, /device:TPU:8, one launch (start us, length us, event | category | flops | bytes accessed | tf_op | source)
XLA Modules:
  0.0 329.9 jit_solution(8823708236835030233)
XLA Ops:
  0.6 0.7 convert_element_type.41
  2.3 52.2 %gather_weights.1 = (bf16[2,2,2,2,144,768]{5,4,3,2,1,0:T(8,128)(2,1)}, bf16[3,144,768]{2,1,0:T(8,128)(2,1)}, bf16[3,144,768]{2,1,0:T(8,128)(2,1)}, bf16[2,2,2,16...) custom-call(s32[8]{0:T(128)} %owners.1, f32[2,144,768]{2,1,0:T(8,128)} %bitcast.50, bf16[16,768]{1,0:T(8,128)(2,1)} %copy-done.16, ...), custom_call_target="tpu_custom_call" | custom-call | tf_op jit(solution)/shard_map/gather_weights/pallas_call | solution.py:311
  54.5 1.6 collective-permute-start
  56.6 1.5 collective-permute-start.1
  58.6 0.8 slice.47
  59.8 0.7 dynamic-slice_reduce_fusion
  60.5 0.8 broadcast_in_dim.18.segk_ref
  61.9 12.1 %project.1 = (bf16[2,768,2048]{2,1,0:T(8,128)(2,1)}, bf16[2,768,256]{2,1,0:T(8,128)(2,1)}, bf16[2,768,256]{2,1,0:T(8,128)(2,1)}) custom-call(bf16[2,2048,768]{2,1,0:T(8,128)(2,1)} %bitcast.48, bf16[2,256,768]{2,1,0:T(8,128)(2,1)} %bitcast.45, bf16[2304,768]{1,0:T(8,128)(2,1)} %bitcast.52, f32[8,768]{1,0:T(8,128)} %stack.40.vec_ref.refs_4_), custom_call_target="tpu_custom_call" | custom-call | flops 6039797760 | bytes 12582912 | tf_op jit(solution)/shard_map/project/pallas_call | solution.py:1300
  74.1 20.6 %attention_forward.2 = (bf16[2,1,12,256,2048]{4,3,2,1,0:T(8,128)(2,1)}, bf16[2,12,256,2048]{3,2,1,0:T(8,128)(2,1)}, bf16[2,8,768,256]{3,2,1,0:T(8,128)(2,1)}, f3...) custom-call(bf16[2,768,2048]{2,1,0:T(8,128)(2,1)} %get-tuple-element.82.q_ref, ...), custom_call_target="tpu_custom_call" | custom-call | flops 1610612736 | bytes 37748736 | tf_op jit(solution)/shard_map/attention_forward/pallas_call | solution.py:1365
  94.7 1.6 collective-permute-start.3
  97.4 20.6 %attention_forward.3 = (bf16[2,1,12,256,2048]{4,3,2,1,0:T(8,128)(2,1)}, bf16[2,12,256,2048]{3,2,1,0:T(8,128)(2,1)}, bf16[2,8,768,256]{3,2,1,0:T(8,128)(2,1)}, f3...) custom-call(bf16[2,768,2048]{2,1,0:T(8,128)(2,1)} %get-tuple-element, ...), custom_call_target="tpu_custom_call", output_to_operand_aliasing={{0}: (6, {}), {1}: (7, {}), {2}: (8, {}), {3}: (9, {}), {4}... | custom-call | flops 1610612736 | bytes 37748736 | tf_op jit(solution)/shard_map/attention_forward/pallas_call | solution.py:1365
  118.1 0.8 copy-done.10
  119.4 74.7 %middle.1 = (bf16[2,256,768]{2,1,0:T(8,128)(2,1)}, bf16[2,2,2,2,768,256]{5,4,3,2,1,0:T(8,128)(2,1)}, f32[2,4,2,2,2,8,256]{6,5,4,3,2,1,0:T(8,128)}, f32[2,256,768...) custom-call(bf16[2,2,2,2,768,256]{5,4,3,2,1,0:T(8,128)(2,1)} %bitcas, ...), custom_call_target="tpu_custom_call" | custom-call | tf_op jit(solution)/shard_map/middle/pallas_call | solution.py:843
  194.1 2.3 collective-permute-start.6
  196.6 25.8 %attention_backward.2 = (bf16[2,1,12,256,2048]{4,3,2,1,0:T(8,128)(2,1)}, bf16[2,8,768,256]{3,2,1,0:T(8,128)(2,1)}, bf16[2,768,256]{2,1,0:T(8,128)(2,1)}, bf16[2,768,256]{2,1,0:T(8,128)(2,1)}, f32[2,768,128]{2,1,0:T(8,128)}) custom-call(bf16[2,12,256,2048]{3,2,1,0:T(8,128)(2,1)} %get-tuple-element.105.e_ref, bf16[2,8,768,256]{3,2,1,0:T(8,128)(2,1)} %bitcast.40, ...), custom_call_target="tpu_custom_call" | custom-call | flops 3221225472 | bytes 25165824 | tf_op jit(solution)/shard_map/attention_backward/pallas_call | solution.py:1440
  222.4 4.0 %collective-permute-done.6 = bf16[2,3,144,768]{3,2,1,0:T(8,128)(2,1)S(1)} collective-permute-done((bf16[2,3,144,768]{3,2,1,0:T(8,128)(2,1)}, bf16[2,3,144,768]{3,2,1,0:T(8,128)(2,1)S(1)}, u32[]{:S(2)}, u32[]{:S(2)}) %collective-permute-start.6) | collective-permute-done | bytes 1327136 | tf_op jit(solution)/shard_map/ppermute | solution.py:1484
  226.6 0.9 copy-done.5
  227.5 1.8 add_convert_fusion.refs_2_
  229.3 1.0 dynamic-slice_bitcast_fusion
  230.3 0.7 collective-permute-start.9
  231.4 1.0 dynamic-slice_bitcast_fusion.1
  232.4 1.3 collective-permute-start.8
  234.3 0.6 gather_fusion
  236.2 11.3 %attention_backward.3 = (bf16[2,1,12,256,2048]{4,3,2,1,0:T(8,128)(2,1)}, bf16[2,8,768,256]{3,2,1,0:T(8,128)(2,1)}, bf16[2,768,256]{2,1,0:T(8,128)(2,1)}, bf16[2,768,256]{2,1,0:T(8,128)(2,1)}, f32[2,768,128]{2,1,0:T(8,128)}) custom-call(bf16[2,12,256,2048]{3,2,1,0:T(8,128)(2,1)} %get-tuple-el, ...), custom_call_target="tpu_custom_call", output_to_operand_aliasing={{0}: (7, {}), {1}: (8, {}), {2}: (9, {}), {3}: (10, {}), {4... | custom-call | flops 3221225472 | bytes 25165824 | tf_op jit(solution)/shard_map/attention_backward/pallas_call | solution.py:1440
  247.5 1.3 collective-permute-done.8.refs_1_
  248.8 0.8 copy-done.14
  249.6 69.2 %tail.1 = (bf16[2,256,768]{2,1,0:T(8,128)(2,1)}, f32[2,144,768]{2,1,0:T(8,128)}, bf16[2,4,36,768]{3,2,1,0:T(8,128)(2,1)}, f32[16,768]{1,0:T(8,128)}) custom-call(s32[8]{0:T(128)} %copy-done, bf16[2,2,2,2,768,256]{5,4,3,2,1,0:T(8,128)(2,1)} %bitcast.43, bf16[2,768,256]{2,1,0:T(8,128)(2,1)} %get-tuple-element.124.dk_hbm, ...), custom_call_target="tpu_custom_call" | custom-call | tf_op jit(solution)/shard_map/tail/pallas_call | solution.py:1217
  318.8 0.8 reshape.125
  319.6 0.7 fusion.2
  320.3 7.8 %update_weights.1 = (f32[2,144,768]{2,1,0:T(8,128)}, f32[2,144,768]{2,1,0:T(8,128)}, f32[2,144,768]{2,1,0:T(8,128)}, f32[2,144,768]{2,1,0:T(8,128)}, bf16[2,144,768]{2,1,0:T(8,128)(2,1)}) custom-call(s32[2]{0:T(128)} %get-tuple-element.206.block_ids, s32[2]{0:T(128)} %get-tuple-element.205.first_column, f32[2]{0:T(128)} %pad_maximum_fusion.fixes, ...), custom_call_target="tpu_custom_call" | custom-call | tf_op jit(solution)/shard_map/update_weights/pallas_call | solution.py:1579
  328.1 0.9 copy.71
  329.0 0.9 copy.72
  (75 shorter events, 6.5 us)
Async XLA Ops:
  1.7 0.6 copy-start.16
  54.5 40.2 %collective-permute-start = (bf16[3,144,768]{2,1,0:T(8,128)(2,1)}, bf16[3,144,768]{2,1,0:T(8,128)(2,1)S(1)}, u32[]{:S(2)}, u32[]{:S(2)}) collective-permute-start(bf16[3,144,768]{2,1,0:T(8,128)(2,1)} %get-tuple-element.99.refs_6_), channel_id=1, source_target_pairs={{0,2},{1,3},{2,0},{3,1},{4,6},{5,7},{6,4},{7,5},{8,10},{9,11},{10,... | collective-permute-start | bytes 1990664 | tf_op jit(solution)/shard_map/ppermute | solution.py:1484
  56.0 62.0 %collective-permute-start.2 = (bf16[3,144,768]{2,1,0:T(8,128)(2,1)}, bf16[3,144,768]{2,1,0:T(8,128)(2,1)S(1)}, u32[]{:S(2)}, u32[]{:S(2)}) collective-permute-start(bf16[3,144,768]{2,1,0:T(8,128)(2,1)} %get-tuple-element.99.refs_6_), channel_id=1, source_target_pairs={{0,4},{1,5},{2,6},{3,7},{4,0},{5,1},{6,2},{7,3},{8,12},{9,13},{10,... | collective-permute-start | bytes 1990664 | tf_op jit(solution)/shard_map/ppermute | solution.py:1484
  56.6 38.2 %collective-permute-start.1 = (bf16[3,144,768]{2,1,0:T(8,128)(2,1)}, bf16[3,144,768]{2,1,0:T(8,128)(2,1)S(1)}, u32[]{:S(2)}, u32[]{:S(2)}) collective-permute-start(bf16[3,144,768]{2,1,0:T(8,128)(2,1)} %get-tuple-element.101.refs_10_), channel_id=1, source_target_pairs={{0,4},{1,5},{2,6},{3,7},{4,0},{5,1},{6,2},{7,3},{8,12},{9,13},{10,... | collective-permute-start | bytes 1990664 | tf_op jit(solution)/shard_map/ppermute | solution.py:1484
  58.1 60.0 %collective-permute-start.4 = (bf16[3,144,768]{2,1,0:T(8,128)(2,1)}, bf16[3,144,768]{2,1,0:T(8,128)(2,1)S(1)}, u32[]{:S(2)}, u32[]{:S(2)}) collective-permute-start(bf16[3,144,768]{2,1,0:T(8,128)(2,1)} %get-tuple-element.101.refs_10_), channel_id=1, source_target_pairs={{0,2},{1,3},{2,0},{3,1},{4,6},{5,7},{6,4},{7,5},{8,10},{9,11},{10,... | collective-permute-start | bytes 1990664 | tf_op jit(solution)/shard_map/ppermute | solution.py:1484
  94.7 23.4 %copy-start.9 = (bf16[3,144,768]{2,1,0:T(8,128)(2,1)}, bf16[3,144,768]{2,1,0:T(8,128)(2,1)S(1)}, u32[]{:S(2)}) copy-start(bf16[3,144,768]{2,1,0:T(8,128)(2,1)S(1)} %collective-permute-done.refs_7_) | copy-start | bytes 1990660
  94.7 23.3 %copy-start.11 = (bf16[3,144,768]{2,1,0:T(8,128)(2,1)}, bf16[3,144,768]{2,1,0:T(8,128)(2,1)S(1)}, u32[]{:S(2)}) copy-start(bf16[3,144,768]{2,1,0:T(8,128)(2,1)S(1)} %collective-permute-done.1.refs_12_) | copy-start | bytes 1990660
  94.7 23.4 %collective-permute-start.3 = (bf16[3,144,768]{2,1,0:T(8,128)(2,1)S(1)}, bf16[3,144,768]{2,1,0:T(8,128)(2,1)S(1)}, u32[]{:S(2)}, u32[]{:S(2)}) collective-permute-start(bf16[3,144,768]{2,1,0:T(8,128)(2,1)S(1)} %collective-permute-done.refs_7_), channel_id=1, source_target_pairs={{0,4},{1,5},{2,6},{3,7},{4,0},{5,1},{6,2},{7,3},{8,12},{9,13},{10,... | collective-permute-start | bytes 1990664 | tf_op jit(solution)/shard_map/ppermute | solution.py:1484
  96.3 21.9 %collective-permute-start.5 = (bf16[3,144,768]{2,1,0:T(8,128)(2,1)S(1)}, bf16[3,144,768]{2,1,0:T(8,128)(2,1)}, u32[]{:S(2)}, u32[]{:S(2)}) collective-permute-start(bf16[3,144,768]{2,1,0:T(8,128)(2,1)S(1)} %collective-permute-done.1.refs_12_), channel_id=1, source_target_pairs={{0,2},{1,3},{2,0},{3,1},{4,6},{5,7},{6,4},{7,5},{8,10},{9,11},{10,... | collective-permute-start | bytes 1990664 | tf_op jit(solution)/shard_map/ppermute | solution.py:1484
  118.1 0.8 copy-start.10
  118.1 1.0 copy-start.12
  118.1 1.2 copy-start.15
  119.4 77.1 %copy-start.20 = (s32[8]{0:T(128)S(1)}, s32[8]{0:T(128)}, u32[]{:S(2)}) copy-start(s32[8]{0:T(128)} %owners.1) | copy-start | bytes 100
  194.1 32.3 %collective-permute-start.6 = (bf16[2,3,144,768]{3,2,1,0:T(8,128)(2,1)}, bf16[2,3,144,768]{3,2,1,0:T(8,128)(2,1)S(1)}, u32[]{:S(2)}, u32[]{:S(2)}) collective-permute-start(bf16[2,3,144,768]{3,2,1,0:T(8,128)(2,1)} %bitcast.67), channel_id=1, source_target_pairs={{0,4},{1,5},{2,6},{3,7},{4,0},{5,1},{6,2},{7,3},{8,12},{9,13},{10,... | collective-permute-start | bytes 3981320 | tf_op jit(solution)/shard_map/ppermute | solution.py:1484
  196.3 30.2 %collective-permute-start.7 = (bf16[2,3,144,768]{3,2,1,0:T(8,128)(2,1)}, bf16[2,3,144,768]{3,2,1,0:T(8,128)(2,1)}, u32[]{:S(2)}, u32[]{:S(2)}) collective-permute-start(bf16[2,3,144,768]{3,2,1,0:T(8,128)(2,1)} %bitcast.66), channel_id=1, source_target_pairs={{0,2},{1,3},{2,0},{3,1},{4,6},{5,7},{6,4},{7,5},{8,10},{9,11},{10,... | collective-permute-start | bytes 3981320 | tf_op jit(solution)/shard_map/ppermute | solution.py:1484
  196.6 37.7 %copy-start = (s32[8]{0:T(128)}, s32[8]{0:T(128)S(1)}, u32[]{:S(2)}) copy-start(s32[8]{0:T(128)S(1)} %select_reduce_fusion.inverse) | copy-start | bytes 100
  196.6 30.9 %copy-start.4 = (bf16[2,3,144,768]{3,2,1,0:T(8,128)(2,1)S(1)}, bf16[2,3,144,768]{3,2,1,0:T(8,128)(2,1)}, u32[]{:S(2)}) copy-start(bf16[2,3,144,768]{3,2,1,0:T(8,128)(2,1)} %get-tuple-element.132) | copy-start | bytes 3981316
  226.4 1.1 copy-start.5
  227.5 3.6 %copy-start.3 = (bf16[2,3,144,768]{3,2,1,0:T(8,128)(2,1)S(1)}, bf16[2,3,144,768]{3,2,1,0:T(8,128)(2,1)}, u32[]{:S(2)}) copy-start(bf16[2,3,144,768]{3,2,1,0:T(8,128)(2,1)} %get-tuple-element.130) | copy-start | bytes 3981316
  227.5 3.6 %copy-start.6 = (bf16[2,3,144,768]{3,2,1,0:T(8,128)(2,1)S(1)}, bf16[2,3,144,768]{3,2,1,0:T(8,128)(2,1)}, u32[]{:S(2)}) copy-start(bf16[2,3,144,768]{3,2,1,0:T(8,128)(2,1)} %copy-done.5) | copy-start | bytes 3981316
  229.3 2.1 copy-start.1
  230.3 17.1 %collective-permute-start.9 = (bf16[3,144,768]{2,1,0:T(8,128)(2,1)}, bf16[3,144,768]{2,1,0:T(8,128)(2,1)S(1)}, u32[]{:S(2)}, u32[]{:S(2)}) collective-permute-start(bf16[3,144,768]{2,1,0:T(8,128)(2,1)} %dynamic-slice_bitcast_fusion), channel_id=1, source_target_pairs={{0,4},{1,5},{2,6},{3,7},{4,0},{5,1},{6,2},{7,3},{8,12},{9,13},{10,... | collective-permute-start | bytes 1990664 | tf_op jit(solution)/shard_map/ppermute | solution.py:1484
  231.4 16.0 %copy-start.2 = (bf16[2,3,144,768]{3,2,1,0:T(8,128)(2,1)}, bf16[2,3,144,768]{3,2,1,0:T(8,128)(2,1)S(1)}, u32[]{:S(2)}) copy-start(bf16[2,3,144,768]{3,2,1,0:T(8,128)(2,1)S(1)} %add_convert_fusion.1.refs_0_) | copy-start | bytes 3981316
  232.4 16.4 %collective-permute-start.8 = (bf16[3,144,768]{2,1,0:T(8,128)(2,1)}, bf16[3,144,768]{2,1,0:T(8,128)(2,1)S(1)}, u32[]{:S(2)}, u32[]{:S(2)}) collective-permute-start(bf16[3,144,768]{2,1,0:T(8,128)(2,1)} %dynamic-slice_bitcast_fusion.1), channel_id=1, source_target_pairs={{0,2},{1,3},{2,0},{3,1},{4,6},{5,7},{6,4},{7,5},{8,10},{9,11},{10,... | collective-permute-start | bytes 1990664 | tf_op jit(solution)/shard_map/ppermute | solution.py:1484
  247.4 1.4 copy-start.13
  248.8 0.8 copy-start.14
  249.6 70.0 %copy-start.17 = (f32[2,144]{1,0:T(2,128)S(1)}, f32[2,144]{1,0:T(2,128)}, u32[]{:S(2)}) copy-start(f32[2,144]{1,0:T(2,128)} %param.21) | copy-start | bytes 3460
  249.6 70.0 %copy-start.18 = (f32[2,144]{1,0:T(2,128)S(1)}, f32[2,144]{1,0:T(2,128)}, u32[]{:S(2)}) copy-start(f32[2,144]{1,0:T(2,128)} %param.23) | copy-start | bytes 3460
  249.6 70.0 %copy-start.19 = (f32[2,144]{1,0:T(2,128)S(1)}, f32[2,144]{1,0:T(2,128)}, u32[]{:S(2)}) copy-start(f32[2,144]{1,0:T(2,128)} %param.22) | copy-start | bytes 3460
  320.3 7.8 %copy-start.7 = (bf16[2,256,768]{2,1,0:T(8,128)(2,1)S(1)}, bf16[2,256,768]{2,1,0:T(8,128)(2,1)}, u32[]{:S(2)}) copy-start(bf16[2,256,768]{2,1,0:T(8,128)(2,1)} %get-tuple-element.103) | copy-start | bytes 2359300
  320.3 8.7 %copy-start.8 = (bf16[2,256,768]{2,1,0:T(8,128)(2,1)S(1)}, bf16[2,256,768]{2,1,0:T(8,128)(2,1)}, u32[]{:S(2)}) copy-start(bf16[2,256,768]{2,1,0:T(8,128)(2,1)} %get-tuple-element.134) | copy-start | bytes 2359300
